TPU v7x, 512 devices: a whole 4x8x8 slice. The times are simulated.
512 devices in a mesh: rows: 64 (over y, x, core), sub: 8 (over z).
Axes of the slice: x: 4, y: 8, z: 8, core: 2. Of those that a mesh axis runs over, the one named last changes fastest.
Arguments:
- stiffness: bfloat16 [16384, 64, 512], P(('rows', 'sub')), may hold values from -0.75 to 0.75
- prolongator: bfloat16 [16384, 64, 64], P(('rows', 'sub')), may hold values from -0.75 to 0.75
- column_index: int32 [16384, 8], P(('rows', 'sub')), may hold values from 0 to 16383, as said below
- slot_index: int32 [16384, 8], P(('rows', 'sub')), may hold values from 0 to 64, as said below
- place_index: int32 [512, 64], P(('rows', 'sub')), may hold values from 0 to 63, as said below
Outputs:
- coarse: float32 [4096, 64, 64], P(('rows', 'sub'))
Inputs may be any that keep to these rules, and one draw needn't show every extreme that they name: column_index[i, 0] = i, and every column lies within 4 rows of the 32 rows of the device that holds row i. `slot_index`: in each row the empty blocks come last, and at least half of a row's blocks are not empty. For each slot j and each s below 8, the devices d with d % 8 == s give place_index[d, j] // 8 each value from 0 to 7 exactly 64 // 8 times.
All inputs are finite; a program needn't handle non-finite values.
Results may differ from a plain program's by a relative error of at most 0.0029.
Values may be sent and summed in bfloat16 or wider, within the bound.
No kernel may reach another device: no remote copies, remote signals or barrier semaphores. Data moves between devices by JAX's collectives and lax.ppermute only.
A program may use at most 64 MiB of HBM per device.

v0:
```python
import jax
import jax.numpy as jnp
from jax import lax
from jax.sharding import PartitionSpec as P

COARSE_DEV = 8
REACH = 4


def extended_2(shard, sides, width):
    edges = {}
    for axis, dim in sides:
        count, length = (lax.axis_size(axis), shard.shape[dim])
        up = [(i, (i + 1) % count) for i in range(count - 1)]
        last = lax.slice_in_dim(shard, length - width, length, axis=dim)
        first = lax.slice_in_dim(shard, 0, width, axis=dim)
        edges[dim] = (
            lax.ppermute(last, axis, up),
            lax.ppermute(first, axis, [(b, a) for a, b in up]),
        )
    done = []
    for _, dim in sides:
        low, high = edges[dim]
        around = [(width, width) if d in done else (0, 0) for d in range(shard.ndim)]
        shard = jnp.concatenate([jnp.pad(low, around), shard, jnp.pad(high, around)], axis=dim)
        done.append(dim)
    return shard


def cut_along(shard, dim, count):
    before, after = (shard.shape[:dim], shard.shape[dim + 1 :])
    return jnp.moveaxis(shard.reshape(*before, count, -1, *after), dim, 0)


def sum_at_owner(shard, axis, dim):
    count = lax.axis_size(axis)
    tiles = lax.all_to_all(cut_along(shard, dim, count), axis, 0, 0, tiled=True)
    return jnp.sum(tiles, axis=0)


def body(stiffness, prolongator, column_index, slot_index, place_index):
    row_count = prolongator.shape[0]
    width = prolongator.shape[1]
    stored = column_index.shape[1]
    owner_count = lax.axis_size("rows")
    group_count = lax.axis_size("sub")
    extended = extended_2(prolongator, ((("rows", "sub"), 0),), REACH)
    device = lax.axis_index(("rows", "sub"))
    local_columns = column_index - device * row_count + REACH
    neighbour = jnp.take(extended, local_columns, axis=0)
    rows_a = stiffness.reshape(row_count, width, stored, width)
    middle = jnp.einsum(
        "rakb,rkbc->rakc", rows_a, neighbour, preferred_element_type=jnp.float32
    ).astype(jnp.bfloat16)
    terms = jnp.einsum("rba,rbkc->rkac", prolongator, middle, preferred_element_type=jnp.float32)
    partial_value = jax.ops.segment_sum(
        terms.reshape(row_count * stored, width, width),
        slot_index.reshape(-1),
        num_segments=owner_count + 1,
    )[:owner_count]
    places = place_index.reshape(owner_count, 1)
    received, got_places = (
        lax.all_to_all(partial_value, "rows", split_axis=0, concat_axis=0, tiled=True),
        lax.all_to_all(places, "rows", split_axis=0, concat_axis=0, tiled=True),
    )
    table_size = COARSE_DEV * group_count
    table = jax.ops.segment_sum(received, got_places[:, 0], num_segments=table_size)
    coarse = sum_at_owner(table, "sub", 0)
    return coarse


def solution(mesh):
    in_specs = (
        P(("rows", "sub"), None, None),
        P(("rows", "sub"), None, None),
        P(("rows", "sub"), None),
        P(("rows", "sub"), None),
        P(("rows", "sub"), None),
    )
    out_specs = P(("rows", "sub"), None, None)
    return jax.shard_map(body, mesh=mesh, in_specs=in_specs, out_specs=out_specs, check_vma=False)
```

profile of v0, /device:TPU:1, one launch (start us, length us, event | category | flops | bytes accessed | tf_op | source)
XLA Modules:
  0.0 180.7 jit_solution(11157492780987846611)
XLA Ops:
  0.0 1.0 fusion.20
  1.0 4.8 %collective-permute-start = (bf16[4,64,64]{2,1,0:T(8,128)(2,1)S(1)}, bf16[4,64,64]{2,1,0:T(8,128)(2,1)S(1)}, u32[]{:S(2)}, u32[]{:S(2)}) collective-permute-start(bf16[4,64,64]{2,1,0:T(8,128)(2,1)S(1)} %get-tuple-element.7), channel_id=1, source_target_pairs={{0,1},{1,2},{2,3},{3,4},{4,5},{5,6},{6,7},{7,8},{8,9},{9,10},{10,1... | collective-permute-start | bytes 98312 | tf_op jit(solution)/shard_map/ppermute | solution.py:18
  5.8 9.1 %collective-permute-start.1 = (bf16[4,64,64]{2,1,0:T(8,128)(2,1)S(1)}, bf16[4,64,64]{2,1,0:T(8,128)(2,1)S(1)}, u32[]{:S(2)}, u32[]{:S(2)}) collective-permute-start(bf16[4,64,64]{2,1,0:T(8,128)(2,1)S(1)} %get-tuple-element.8), channel_id=1, source_target_pairs={{1,0},{2,1},{3,2},{4,3},{5,4},{6,5},{7,6},{8,7},{9,8},{10,9},{11,1... | collective-permute-start | bytes 98312 | tf_op jit(solution)/shard_map/ppermute | solution.py:19
  14.9 1.4 copy.25
  16.3 10.2 %all-to-all-start = ((s32[64,1,1]{2,1,0:T(1,128)}), s32[64,1,1]{2,1,0:T(1,128)S(1)}, u32[]{:S(2)}, u32[]{:S(2)}) async-start(s32[64,1,1]{2,1,0:T(1,128)} %copy.25), calls=%async_computation | async-start | bytes 65536 | tf_op jit(solution)/shard_map/all_to_all | solution.py:64
  27.5 6.2 %reshape.18 = bf16[32,64,8,64]{3,2,1,0:T(8,128)(2,1)} reshape(bf16[32,64,512]{2,1,0:T(8,128)(2,1)} %param.5) | data formatting | bytes 4194304 | tf_op jit(solution)/shard_map/reshape | solution.py:51
  34.1 3.0 %gather_fusion = bf16[256,64,64]{2,1,0:T(8,128)(2,1)} fusion(bf16[40,64,64]{2,1,0:T(8,128)(2,1)S(1)} %pad_maximum_fusion, s32[1024]{0:T(1024)S(1)} %pad_clamp_fusion), kind=kCustom, calls=%fused_computation | custom fusion | bytes 4195328 | tf_op jit(solution)/shard_map/jit(_take)/gather | solution.py:50
  37.1 6.3 %copy.29 = bf16[32,8,64,64]{2,3,1,0:T(8,128)(2,1)} copy(bf16[32,8,64,64]{3,2,1,0:T(8,128)(2,1)} %bitcast.16) | data formatting | bytes 4194304 | tf_op jit(solution)/shard_map/jit(_take)/gather | solution.py:50
  43.5 7.9 %fusion = f32[32,8,64,64]{3,2,1,0:T(8,128)} fusion(bf16[32,64,8,64]{3,2,1,0:T(8,128)(2,1)} %reshape.18, bf16[32,8,64,64]{2,3,1,0:T(8,128)(2,1)} %copy.29, pred[32,8]{1,0:T(8,128)(4,1)S(1)} %copy.27, bf16[32,64,64]{2,1,0:T(8,128)(2,1)S(1)} %copy-done), kind=kOutput, calls=%fused_computation.3 | convolution fusion | flops 270532608 | bytes 8651008 | tf_op jit(solution)/shard_map/rba,rbkc->rkac/dot_general | solution.py:55
  51.4 9.0 %copy.31 = f32[256,64,64]{2,1,0:T(8,128)} copy(f32[256,64,64]{1,2,0:T(8,128)} %bitcast.14) | data formatting | bytes 8388608 | tf_op jit(solution)/shard_map/reshape | solution.py:57
  60.6 26.2 %scatter_fusion = f32[65,64,64]{2,1,0:T(8,128)S(1)} fusion(f32[65,64,64]{2,1,0:T(8,128)S(1)} %broadcast_in_dim.19, s32[256]{0:T(256)S(1)} %reshape.31, f32[256,64,64]{2,1,0:T(8,128)} %copy.31), kind=kCustom, calls=%fused_computation.1 | custom fusion | flops 1048576 | bytes 12583936 | tf_op jit(solution)/shard_map/scatter-add | solution.py:56
  86.8 1.5 slice.14
  88.3 3.4 %reshape.51 = f32[64,1,4096]{2,1,0:T(1,128)} reshape(f32[64,64,64]{2,1,0:T(8,128)} %slice.14) | data formatting | bytes 2097152
  91.7 10.3 %all-to-all-start.1 = ((f32[64,1,4096]{2,1,0:T(1,128)}), f32[64,1,4096]{2,1,0:T(1,128)S(1)}, u32[]{:S(2)}, u32[]{:S(2)}) async-start(f32[64,1,4096]{2,1,0:T(1,128)} %reshape.51), calls=%async_computation.1 | async-start | bytes 2097152 | tf_op jit(solution)/shard_map/all_to_all | solution.py:63
  102.0 1.2 reduce
  103.3 26.9 %all-to-all-done.1 = f32[64,1,4096]{2,1,0:T(1,128)S(1)} async-done(((f32[64,1,4096]{2,1,0:T(1,128)}), f32[64,1,4096]{2,1,0:T(1,128)S(1)}, u32[]{:S(2)}, u32[]{:S(2)}) %all-to-all-start.1) | async-done | bytes 1048608 | tf_op jit(solution)/shard_map/all_to_all | solution.py:63
  130.7 3.3 %reduce.1 = f32[64,4096]{1,0:T(8,128)S(1)} reduce(f32[64,1,4096]{2,1,0:T(1,128)S(1)} %all-to-all-done.1, f32[]{:T(128)} %broadcast.9), dimensions={1}, to_apply=%all_to_all.17.reduce_sub_computation | reduce | bytes 2097156 | tf_op jit(solution)/shard_map/all_to_all | solution.py:63
  134.0 2.2 %reshape.52 = f32[64,64,64]{2,1,0:T(8,128)} reshape(f32[64,4096]{1,0:T(8,128)S(1)} %reduce.1) | data formatting | bytes 2097152
  136.4 7.0 %scatter_fusion.1 = f32[64,64,64]{2,1,0:T(8,128)S(1)} fusion(f32[64,64,64]{2,1,0:T(8,128)S(1)} %broadcast_in_dim.18, s32[64]{0:T(128)S(1)} %reduce, f32[64,64,64]{2,1,0:T(8,128)} %reshape.52), kind=kCustom, calls=%fused_computation.2 | custom fusion | flops 262144 | bytes 3145984 | tf_op jit(solution)/shard_map/scatter-add | solution.py:67
  143.4 1.3 reshape.53
  144.8 31.0 %all_to_all.22 = f32[8,1,32768]{2,1,0:T(1,128)S(1)} all-to-all(f32[8,1,32768]{2,1,0:T(1,128)S(1)} %reshape.53), channel_id=1, replica_groups=mesh['rows'=64,'sub'=8] {'sub'}, dimensions={0} | all-to-all | bytes 2097152 | tf_op jit(solution)/shard_map/all_to_all | solution.py:37
  175.8 3.1 %reduce.2 = f32[8,32768]{1,0:T(8,128)S(1)} reduce(f32[8,1,32768]{2,1,0:T(1,128)S(1)} %all_to_all.22, f32[]{:T(128)} %broadcast.9), dimensions={1}, to_apply=%all_to_all.18.reduce_sub_computation | reduce | bytes 2097156 | tf_op jit(solution)/shard_map/all_to_all | solution.py:37
  178.9 0.8 reshape.54
  179.8 0.9 reduce_sum.9
  (18 shorter events, 2.3 us)
Async XLA Ops:
  0.0 33.9 %copy-start = (bf16[32,64,64]{2,1,0:T(8,128)(2,1)S(1)}, bf16[32,64,64]{2,1,0:T(8,128)(2,1)}, u32[]{:S(2)}) copy-start(bf16[32,64,64]{2,1,0:T(8,128)(2,1)} %param.6) | copy-start | bytes 786436
  0.0 33.7 %copy-start.1 = (s32[32,8]{0,1:T(8,128)S(1)}, s32[32,8]{0,1:T(8,128)}, u32[]{:S(2)}) copy-start(s32[32,8]{0,1:T(8,128)} %param.8) | copy-start | bytes 3076
  1.0 33.0 %collective-permute-start = (bf16[4,64,64]{2,1,0:T(8,128)(2,1)S(1)}, bf16[4,64,64]{2,1,0:T(8,128)(2,1)S(1)}, u32[]{:S(2)}, u32[]{:S(2)}) collective-permute-start(bf16[4,64,64]{2,1,0:T(8,128)(2,1)S(1)} %get-tuple-element.7), channel_id=1, source_target_pairs={{0,1},{1,2},{2,3},{3,4},{4,5},{5,6},{6,7},{7,8},{8,9},{9,10},{10,1... | collective-permute-start | bytes 98312 | tf_op jit(solution)/shard_map/ppermute | solution.py:18
  5.8 28.1 %collective-permute-start.1 = (bf16[4,64,64]{2,1,0:T(8,128)(2,1)S(1)}, bf16[4,64,64]{2,1,0:T(8,128)(2,1)S(1)}, u32[]{:S(2)}, u32[]{:S(2)}) collective-permute-start(bf16[4,64,64]{2,1,0:T(8,128)(2,1)S(1)} %get-tuple-element.8), channel_id=1, source_target_pairs={{1,0},{2,1},{3,2},{4,3},{5,4},{6,5},{7,6},{8,7},{9,8},{10,9},{11,1... | collective-permute-start | bytes 98312 | tf_op jit(solution)/shard_map/ppermute | solution.py:19
  16.3 75.4 %all-to-all-start = ((s32[64,1,1]{2,1,0:T(1,128)}), s32[64,1,1]{2,1,0:T(1,128)S(1)}, u32[]{:S(2)}, u32[]{:S(2)}) async-start(s32[64,1,1]{2,1,0:T(1,128)} %copy.25), calls=%async_computation | async-start | bytes 65536 | tf_op jit(solution)/shard_map/all_to_all | solution.py:64
  91.7 38.5 %all-to-all-start.1 = ((f32[64,1,4096]{2,1,0:T(1,128)}), f32[64,1,4096]{2,1,0:T(1,128)S(1)}, u32[]{:S(2)}, u32[]{:S(2)}) async-start(f32[64,1,4096]{2,1,0:T(1,128)} %reshape.51), calls=%async_computation.1 | async-start | bytes 2097152 | tf_op jit(solution)/shard_map/all_to_all | solution.py:63
where the time goes:
time: 184 us; the launch traced here: 181 us
  other arithmetic  42.6 us (23%)
  local copies, waits for them, and re-layouts  37.6 us (20%)
  starting transfers between devices  34.5 us (19%)
  blocking collectives  31 us (17%)
  waiting for transfers between devices  26.9 us (15%)
  matrix products  7.94 us (4%)
    all_to_all x1, blocking collectives, sum_at_owner(): tiles = lax.all_to_all(cut_along(shard, dim, count), axis, 0, 0, tiled=True)  31 us
    all_to_all x1, waiting for transfers between devices, body(): lax.all_to_all(partial_value, 'rows', split_axis=0, concat_axis=0, tiled=...  26.9 us
    scatter-add x1, other arithmetic, body(): jax.ops.segment_sum(terms.reshape(row_count * stored, width, width), slot...  26.2 us
    all_to_all x1, starting transfers between devices, body(): lax.all_to_all(partial_value, 'rows', split_axis=0, concat_axis=0, tiled=...  10.3 us
    all_to_all x1, starting transfers between devices, body(): lax.all_to_all(places, 'rows', split_axis=0, concat_axis=0, tiled=True)  10.2 us
    gather x2, local copies, waits for them, and re-layouts, body(): neighbour = jnp.take(extended, local_columns, axis=0)  9.37 us
    ppermute x1, starting transfers between devices, extended_2(): lax.ppermute(first, axis, [(b, a) for a, b in up])  9.15 us
    reshape x1, local copies, waits for them, and re-layouts, body(): terms.reshape(row_count * stored, width, width)  8.97 us
  transfers between devices with their start and end apart: 4, of which 1 were waited for; matrix products, arithmetic and copies ran while one was open for 37% of the time, Pallas kernels for 0%

commit v1 on v0

v1 whole, which is shorter than its diff:
```python
import jax
import jax.numpy as jnp
from jax import lax
from jax.experimental import pallas as pl
from jax.experimental.pallas import tpu as pltpu
from jax.sharding import PartitionSpec as P

COARSE_DEV = 8
REACH = 4
LANES = 128
STEPS = 4
NOTE = 8


def product_kernel(cols, slots, places, a_ref, own_ref, low_ref, high_ref, out_ref, left, right, own_t, even, odd):
    step = pl.program_id(0)
    owners, packed, _ = out_ref.shape
    half = (packed - NOTE)
    width = own_ref.shape[1]
    rows_own = own_ref.shape[0]
    rows_step, stored = a_ref.shape[0], cols.shape[0]

    @pl.when(step == 0)
    def _():
        zero = jnp.zeros((width, width), own_ref.dtype)

        def place(index, block):
            left[index] = jnp.concatenate([block, zero], axis=1)
            right[index] = jnp.concatenate([zero, block], axis=1)

        for n in range(REACH):
            place(n, low_ref[n])
            place(REACH + rows_own + n, high_ref[n])

        @pl.loop(0, rows_own)
        def _(n):
            block = own_ref[n]
            place(REACH + n, block)
            own_t[n] = block.T

        @pl.loop(0, even.shape[0])
        def _(n):
            even[n] = jnp.zeros(even.shape[1:], even.dtype)
            odd[n] = jnp.zeros(odd.shape[1:], odd.dtype)

    base = cols[0, 0] - REACH

    @pl.loop(0, rows_step)
    def _(n):
        row = step * rows_step + n
        middles = []
        for k in range(0, stored, 2):
            sides = jnp.concatenate([left[cols[k, row] - base], right[cols[k + 1, row] - base]], axis=0)
            pair = jnp.dot(a_ref[n, :, k * width:(k + 2) * width], sides, preferred_element_type=jnp.float32)
            middles.append(pair.astype(jnp.bfloat16))
        terms = jnp.dot(own_t[row], jnp.concatenate(middles, axis=1), preferred_element_type=jnp.float32)
        for k in range(0, stored, 2):
            pair = terms[:, k * width:(k + 2) * width]
            even[slots[k, row]] += pair
            odd[slots[k + 1, row]] += pair

    @pl.when(step == pl.num_programs(0) - 1)
    def _():
        lane = lax.broadcasted_iota(jnp.int32, (half, LANES), 1)

        @pl.loop(0, owners)
        def _(j):
            e, o = even[j], odd[j]
            top = e[:half] + pltpu.roll(o[:half], width, 1)
            low = pltpu.roll(e[half:], width, 1) + o[half:]
            out_ref[j, :half] = jnp.where(lane < width, top, low).astype(out_ref.dtype)
            out_ref[j, half:] = jnp.full((NOTE, LANES), places[0, j].astype(jnp.float32), jnp.float32).astype(out_ref.dtype)


def route_kernel(in_ref, out_ref, count):
    blocks, packed, _ = in_ref.shape
    half = packed - NOTE
    groups = out_ref.shape[0]
    each = blocks // groups
    for g in range(groups):
        count[g] = 0
    for n in range(blocks):
        place = in_ref[n, half:].astype(jnp.float32)[0, 0].astype(jnp.int32)
        g = place // COARSE_DEV
        rank = count[g]
        count[g] = rank + 1
        out_ref[g, rank] = in_ref[n]


def sum_kernel(in_ref, out_ref, total):
    groups, each, packed, _ = in_ref.shape
    half = packed - NOTE
    width = out_ref.shape[2]
    total[...] = jnp.zeros_like(total)
    for g in range(groups):
        for n in range(each):
            place = in_ref[g, n, half:].astype(jnp.float32)[0, 0].astype(jnp.int32)
            total[place % COARSE_DEV] += in_ref[g, n, :half].astype(jnp.float32)
    for n in range(out_ref.shape[0]):
        block = total[n]
        out_ref[n, :half] = block[:, :width]
        out_ref[n, half:] = block[:, width:]


def body(stiffness, prolongator, column_index, slot_index, place_index):
    row_count, width, _ = prolongator.shape
    stored = column_index.shape[1]
    owners, groups = lax.axis_size("rows"), lax.axis_size("sub")
    axes = ("rows", "sub")
    count = owners * groups
    up = [(i, i + 1) for i in range(count - 1)]
    low = lax.ppermute(prolongator[row_count - REACH:], axes, up)
    high = lax.ppermute(prolongator[:REACH], axes, [(b, a) for a, b in up])
    half = width * width // LANES
    packed = half + NOTE
    smem = pl.BlockSpec(memory_space=pltpu.SMEM)
    vmem = pl.BlockSpec(memory_space=pltpu.VMEM)
    rows_step = row_count // STEPS
    sent = pl.pallas_call(
        product_kernel,
        grid=(STEPS,),
        out_shape=jax.ShapeDtypeStruct((owners, packed, LANES), jnp.bfloat16),
        in_specs=[smem, smem, smem, pl.BlockSpec((rows_step, width, stored * width), lambda n: (n, 0, 0)), vmem, vmem, vmem],
        out_specs=vmem,
        scratch_shapes=[
            pltpu.VMEM((row_count + 2 * REACH, width, LANES), jnp.bfloat16),
            pltpu.VMEM((row_count + 2 * REACH, width, LANES), jnp.bfloat16),
            pltpu.VMEM((row_count, width, width), jnp.bfloat16),
            pltpu.VMEM((owners + 1, width, LANES), jnp.float32),
            pltpu.VMEM((owners + 1, width, LANES), jnp.float32),
        ],
        name="product",
    )(column_index.T, slot_index.T, place_index, stiffness, prolongator, low, high)
    received = lax.all_to_all(sent, "rows", 0, 0, tiled=True)
    routed = pl.pallas_call(
        route_kernel,
        out_shape=jax.ShapeDtypeStruct((groups, owners // groups, packed, LANES), jnp.bfloat16),
        in_specs=[vmem],
        out_specs=vmem,
        scratch_shapes=[pltpu.SMEM((groups,), jnp.int32)],
        name="route",
    )(received)
    gathered = lax.all_to_all(routed, "sub", 0, 0, tiled=True)
    return pl.pallas_call(
        sum_kernel,
        out_shape=jax.ShapeDtypeStruct((COARSE_DEV, width, width), jnp.float32),
        in_specs=[vmem],
        out_specs=vmem,
        scratch_shapes=[pltpu.VMEM((COARSE_DEV, half, LANES), jnp.float32)],
        name="total",
    )(gathered)


def solution(mesh):
    split = ("rows", "sub")
    in_specs = (P(split, None, None), P(split, None, None), P(split, None), P(split, None), P(split, None))
    return jax.shard_map(body, mesh=mesh, in_specs=in_specs, out_specs=P(split, None, None), check_vma=False)
```

time: 184 us -> 104 us (0.57); the launches traced: 181 us -> 104 us
  other arithmetic: 42.6 us -> 0 us
  local copies, waits for them, and re-layouts: 37.6 us -> 1.51 us
  blocking collectives: 31 us -> 57.6 us
  Pallas kernels: 0 us -> 25 us
  waiting for transfers between devices: 26.9 us -> 5.51 us
  starting transfers between devices: 34.5 us -> 14 us
  matrix products: 7.94 us -> 0 us
    scatter-add x2 -> x0, other arithmetic: 33.2 us -> none  [the longest x1 26.2 us: body(): jax.ops.segment_sum(terms.reshape(row_count * stored, width, width), slot...]
    all_to_all x2 -> x0, waiting for transfers between devices: 26.9 us -> none  [the longest x1 26.9 us: body(): lax.all_to_all(partial_value, 'rows', split_axis=0, concat_axis=0, tiled=...]
    all_to_all x1 -> x2, blocking collectives: 31 us -> 57.6 us  [the longest x1 33.6 us: body(): received = lax.all_to_all(sent, 'rows', 0, 0, tiled=True)]
    pallas_call x0 -> x3, Pallas kernels: none -> 25 us  [the longest x1 20.2 us: body(): pl.pallas_call(product_kernel, grid=(STEPS,), out_shape=jax.ShapeDtypeStr...]
    all_to_all x2 -> x0, starting transfers between devices: 20.5 us -> none  [the longest x1 10.3 us: body(): lax.all_to_all(partial_value, 'rows', split_axis=0, concat_axis=0, tiled=...]
    reshape x2 -> x0, local copies, waits for them, and re-layouts: 15.2 us -> none  [the longest x1 8.97 us: body(): terms.reshape(row_count * stored, width, width)]
    gather x2 -> x0, local copies, waits for them, and re-layouts: 9.37 us -> none  [body(): neighbour = jnp.take(extended, local_columns, axis=0)]
    dot_general x1 -> x0, matrix products: 7.94 us -> none  [body(): jnp.einsum('rba,rbkc->rkac', prolongator, middle, preferred_element_type=...]
  transfers between devices with their start and end apart: 4 -> 2, of which waited for: 1 -> 1; matrix products, arithmetic and copies ran while one was open for 37% -> 0% of each run, Pallas kernels for 0% -> 0%
where the time goes in v1:
time: 104 us
  blocking collectives  57.6 us (55%)
  Pallas kernels  25 us (24%)
  starting transfers between devices  14 us (13%)
  waiting for transfers between devices  5.51 us (5%)
  local copies, waits for them, and re-layouts  1.51 us (1%)
    all_to_all x1, blocking collectives, body(): received = lax.all_to_all(sent, 'rows', 0, 0, tiled=True)  33.6 us
    all_to_all x1, blocking collectives, body(): gathered = lax.all_to_all(routed, 'sub', 0, 0, tiled=True)  24 us
    pallas_call x1, Pallas kernels, body(): pl.pallas_call(product_kernel, grid=(STEPS,), out_shape=jax.ShapeDtypeStr...  20.2 us
    ppermute x1, starting transfers between devices, body(): high = lax.ppermute(prolongator[:REACH], axes, [(b, a) for a, b in up])  12 us
    ppermute x1, waiting for transfers between devices, body(): low = lax.ppermute(prolongator[row_count - REACH:], axes, up)  5.5 us
    pallas_call x1, Pallas kernels, body(): pl.pallas_call(route_kernel, out_shape=jax.ShapeDtypeStruct((groups, owne...  2.49 us
    pallas_call x1, Pallas kernels, body(): pl.pallas_call(sum_kernel, out_shape=jax.ShapeDtypeStruct((COARSE_DEV, wi...  2.29 us
  transfers between devices with their start and end apart: 2, of which 1 were waited for; matrix products, arithmetic and copies ran while one was open for 0% of the time, Pallas kernels for 0%

profile of v1, /device:TPU:1, one launch (start us, length us, event | category | flops | bytes accessed | tf_op | source)
XLA Modules:
  0.0 103.6 jit_solution(6103533754391693970)
XLA Ops:
  0.0 0.9 fusion
  0.9 12.0 %collective-permute-start.1 = (bf16[4,64,64]{2,1,0:T(8,128)(2,1)S(1)}, bf16[4,64,64]{2,1,0:T(8,128)(2,1)S(1)}, u32[]{:S(2)}, u32[]{:S(2)}) collective-permute-start(bf16[4,64,64]{2,1,0:T(8,128)(2,1)S(1)} %get-tuple-element.5), channel_id=1, source_target_pairs={{1,0},{2,1},{3,2},{4,3},{5,4},{6,5},{7,6},{8,7},{9,8},{10,9},{11,1... | collective-permute-start | bytes 98312 | tf_op jit(solution)/shard_map/ppermute | solution.py:113
  12.9 1.9 %collective-permute-start = (bf16[4,64,64]{2,1,0:T(8,128)(2,1)S(1)}, bf16[4,64,64]{2,1,0:T(8,128)(2,1)S(1)}, u32[]{:S(2)}, u32[]{:S(2)}) collective-permute-start(bf16[4,64,64]{2,1,0:T(8,128)(2,1)S(1)} %get-tuple-element.6), channel_id=1, source_target_pairs={{0,1},{1,2},{2,3},{3,4},{4,5},{5,6},{6,7},{7,8},{8,9},{9,10},{10,1... | collective-permute-start | bytes 98312 | tf_op jit(solution)/shard_map/ppermute | solution.py:112
  14.9 0.0 collective-permute-done.1.high_ref
  14.9 0.0 copy-start
  14.9 5.5 %collective-permute-done.low_ref = bf16[4,64,64]{2,1,0:T(8,128)(2,1)S(1)} collective-permute-done((bf16[4,64,64]{2,1,0:T(8,128)(2,1)S(1)}, bf16[4,64,64]{2,1,0:T(8,128)(2,1)S(1)}, u32[]{:S(2)}, u32[]{:S(2)}) %collective-permute-start) | collective-permute-done | bytes 32800 | tf_op jit(solution)/shard_map/ppermute | solution.py:112
  20.4 0.0 copy-start.1
  20.4 0.0 copy-done
  20.4 0.6 copy-done.1
  21.0 20.2 %product.1 = bf16[64,40,128]{2,1,0:T(8,128)(2,1)} custom-call(s32[8,32]{1,0:T(8,128)} %bitcast.2, s32[8,32]{1,0:T(8,128)} %bitcast.3, s32[1,64]{1,0:T(1,128)} %places.1, bf16[32,64,512]{2,1,0:T(8,128)(2,1)} %a_ref.1, bf16[32,64,64]{2,1,0:T(8,128)(2,1)} %own_ref.1, bf16[4,64,64]{2,1,0:T(8,128)(2,1)} %copy-done.1, bf16[4,64,64]{2,1,0:T(8,128)(2,1)} %copy-done), custom_call_target="tpu_custom_call" | custom-call | tf_op jit(solution)/shard_map/product/pallas_call | solution.py:119
  41.3 33.6 %all_to_all.10.in_ref = bf16[64,40,128]{2,1,0:T(8,128)(2,1)} all-to-all(bf16[64,40,128]{2,1,0:T(8,128)(2,1)} %product.1), channel_id=1, replica_groups=mesh['rows'=64,'sub'=8] {'rows'}, dimensions={0} | all-to-all | bytes 1310720 | tf_op jit(solution)/shard_map/all_to_all | solution.py:134
  74.8 2.5 %route.1 = bf16[8,8,40,128]{3,2,1,0:T(8,128)(2,1)} custom-call(bf16[64,40,128]{2,1,0:T(8,128)(2,1)} %all_to_all.10.in_ref), custom_call_target="tpu_custom_call" | custom-call | tf_op jit(solution)/shard_map/route/pallas_call | solution.py:135
  77.3 24.0 %all_to_all.11.in_ref = bf16[8,8,40,128]{3,2,1,0:T(8,128)(2,1)} all-to-all(bf16[8,8,40,128]{3,2,1,0:T(8,128)(2,1)} %route.1), channel_id=1, replica_groups=mesh['rows'=64,'sub'=8] {'sub'}, dimensions={0} | all-to-all | bytes 1310720 | tf_op jit(solution)/shard_map/all_to_all | solution.py:143
  101.3 2.3 %total.1 = f32[8,64,64]{2,1,0:T(8,128)} custom-call(bf16[8,8,40,128]{3,2,1,0:T(8,128)(2,1)} %all_to_all.11.in_ref), custom_call_target="tpu_custom_call" | custom-call | tf_op jit(solution)/shard_map/total/pallas_call | solution.py:144
Async XLA Ops:
  0.9 14.0 %collective-permute-start.1 = (bf16[4,64,64]{2,1,0:T(8,128)(2,1)S(1)}, bf16[4,64,64]{2,1,0:T(8,128)(2,1)S(1)}, u32[]{:S(2)}, u32[]{:S(2)}) collective-permute-start(bf16[4,64,64]{2,1,0:T(8,128)(2,1)S(1)} %get-tuple-element.5), channel_id=1, source_target_pairs={{1,0},{2,1},{3,2},{4,3},{5,4},{6,5},{7,6},{8,7},{9,8},{10,9},{11,1... | collective-permute-start | bytes 98312 | tf_op jit(solution)/shard_map/ppermute | solution.py:113
  12.9 7.5 %collective-permute-start = (bf16[4,64,64]{2,1,0:T(8,128)(2,1)S(1)}, bf16[4,64,64]{2,1,0:T(8,128)(2,1)S(1)}, u32[]{:S(2)}, u32[]{:S(2)}) collective-permute-start(bf16[4,64,64]{2,1,0:T(8,128)(2,1)S(1)} %get-tuple-element.6), channel_id=1, source_target_pairs={{0,1},{1,2},{2,3},{3,4},{4,5},{5,6},{6,7},{7,8},{8,9},{9,10},{10,1... | collective-permute-start | bytes 98312 | tf_op jit(solution)/shard_map/ppermute | solution.py:112
  14.9 5.5 %copy-start = (bf16[4,64,64]{2,1,0:T(8,128)(2,1)}, bf16[4,64,64]{2,1,0:T(8,128)(2,1)S(1)}, u32[]{:S(2)}) copy-start(bf16[4,64,64]{2,1,0:T(8,128)(2,1)S(1)} %collective-permute-done.1.high_ref) | copy-start | bytes 98308
  20.4 0.6 copy-start.1

commit v2 on v1

v2 whole, which is shorter than its diff:
```python
import jax
import jax.numpy as jnp
from jax import lax
from jax.experimental import pallas as pl
from jax.experimental.pallas import tpu as pltpu
from jax.sharding import PartitionSpec as P

COARSE_DEV = 8
REACH = 4
LANES = 128
BATCH = 16
VMEM_PRODUCT = 60 << 20
VMEM_SMALL = 8 << 20
STEPS = 2
NOTE = 8


def product_kernel(cols, slots, places, a_ref, own_ref, first_ref, second_ref, out_ref, left, right, own_t, even, odd):
    step = pl.program_id(0)
    owners, packed, _ = out_ref.shape
    half = (packed - NOTE)
    width = own_ref.shape[1]
    rows_own = own_ref.shape[0]
    rows_step, stored = a_ref.shape[0], cols.shape[0]

    @pl.when(step == 0)
    def _():
        zero = jnp.zeros((width, width), own_ref.dtype)

        def place(index, block):
            left[index] = jnp.concatenate([block, zero], axis=1)
            right[index] = jnp.concatenate([zero, block], axis=1)

        odd_device = (cols[0, 0] // rows_own) % 2
        above, below = REACH + rows_own, 0
        for n in range(REACH):
            place(above + odd_device * (below - above) + n, first_ref[n])
            place(below + odd_device * (above - below) + n, second_ref[n])

        for n in range(rows_own):
            block = own_ref[n]
            place(REACH + n, block)
            own_t[n] = block.T
        for n in range(even.shape[0]):
            even[n] = jnp.zeros(even.shape[1:], even.dtype)
            odd[n] = jnp.zeros(odd.shape[1:], odd.dtype)

    base = cols[0, 0] - REACH

    first = step * rows_step
    middle = []
    for n in range(rows_step):
        pairs = []
        for k in range(0, stored, 2):
            sides = jnp.concatenate([left[cols[k, first + n] - base], right[cols[k + 1, first + n] - base]], axis=0)
            pair = jnp.dot(a_ref[n, :, k * width:(k + 2) * width], sides, preferred_element_type=jnp.float32)
            pairs.append(pair.astype(jnp.bfloat16))
        middle.append(jnp.concatenate(pairs, axis=1))
    terms = [jnp.dot(own_t[first + n], middle[n], preferred_element_type=jnp.float32) for n in range(rows_step)]
    for n in range(rows_step):
        for k in range(0, stored, 2):
            pair = terms[n][:, k * width:(k + 2) * width]
            even[slots[k, first + n]] += pair
            odd[slots[k + 1, first + n]] += pair

    @pl.when(step == pl.num_programs(0) - 1)
    def _():
        lane = lax.broadcasted_iota(jnp.int32, (half, LANES), 1)

        @pl.loop(0, owners // BATCH)
        def _(part):
            for n in range(BATCH):
                j = part * BATCH + n
                e, o = even[j], odd[j]
                top = e[:half] + pltpu.roll(o[:half], width, 1)
                low = pltpu.roll(e[half:], width, 1) + o[half:]
                out_ref[j, :half] = jnp.where(lane < width, top, low).astype(out_ref.dtype)
                out_ref[j, half:] = jnp.full((NOTE, LANES), places[0, j].astype(jnp.float32), jnp.float32).astype(out_ref.dtype)


def route_kernel(in_ref, out_ref, count):
    blocks, packed, _ = in_ref.shape
    half = packed - NOTE
    groups, length, _ = out_ref.shape
    note_row = lax.broadcasted_iota(jnp.int32, (NOTE, LANES), 0)
    for g in range(groups):
        count[g] = 0
        out_ref[g, length - NOTE:] = jnp.zeros((NOTE, LANES), out_ref.dtype)
    for n in range(blocks):
        note = in_ref[n, half:]
        g = note.astype(jnp.float32)[0, 0].astype(jnp.int32) // COARSE_DEV
        rank = count[g]
        count[g] = rank + 1
        out_ref[g, pl.ds(pl.multiple_of(rank * half, half), half)] = in_ref[n, :half]
        old = out_ref[g, length - NOTE:]
        out_ref[g, length - NOTE:] = jnp.where(note_row == rank, note.astype(jnp.float32), old.astype(jnp.float32)).astype(old.dtype)


def sum_kernel(in_ref, out_ref, total):
    groups, length, _ = in_ref.shape
    half, width = out_ref.shape[1] // 2, out_ref.shape[2]
    total[...] = jnp.zeros_like(total)
    for g in range(groups):
        notes = in_ref[g, length - NOTE:].astype(jnp.float32)
        for n in range(length // half):
            place = notes[n, 0].astype(jnp.int32)
            total[place % COARSE_DEV] += in_ref[g, n * half:(n + 1) * half].astype(jnp.float32)
    for n in range(out_ref.shape[0]):
        block = total[n]
        out_ref[n, :half] = block[:, :width]
        out_ref[n, half:] = block[:, width:]


def body(stiffness, prolongator, column_index, slot_index, place_index):
    row_count, width, _ = prolongator.shape
    stored = column_index.shape[1]
    owners, groups = lax.axis_size("rows"), lax.axis_size("sub")
    axes = ("rows", "sub")
    count = owners * groups
    odd = lax.axis_index("sub") % 2
    tail = row_count - REACH
    first_edge = lax.dynamic_slice_in_dim(prolongator, tail * (1 - odd), REACH, 0)
    second_edge = lax.dynamic_slice_in_dim(prolongator, tail * odd, REACH, 0)
    first = lax.ppermute(first_edge, axes, [(i, i ^ 1) for i in range(count)])
    second = lax.ppermute(second_edge, axes, [(i, ((i + 1) ^ 1) - 1) for i in range(1, count - 1)])
    half = width * width // LANES
    packed = half + NOTE
    length = owners // groups * half + NOTE
    smem = pl.BlockSpec(memory_space=pltpu.SMEM)
    vmem = pl.BlockSpec(memory_space=pltpu.VMEM)
    rows_step = row_count // STEPS
    sent = pl.pallas_call(
        product_kernel,
        grid=(STEPS,),
        out_shape=jax.ShapeDtypeStruct((owners, packed, LANES), jnp.bfloat16),
        in_specs=[smem, smem, smem, pl.BlockSpec((rows_step, width, stored * width), lambda n: (n, 0, 0)), vmem, vmem, vmem],
        out_specs=vmem,
        scratch_shapes=[
            pltpu.VMEM((row_count + 2 * REACH, width, LANES), jnp.bfloat16),
            pltpu.VMEM((row_count + 2 * REACH, width, LANES), jnp.bfloat16),
            pltpu.VMEM((row_count, width, width), jnp.bfloat16),
            pltpu.VMEM((owners + 1, width, LANES), jnp.float32),
            pltpu.VMEM((owners + 1, width, LANES), jnp.float32),
        ],
        compiler_params=pltpu.CompilerParams(vmem_limit_bytes=VMEM_PRODUCT),
        name="product",
    )(column_index.T, slot_index.T, place_index, stiffness, prolongator, first, second)
    received = lax.all_to_all(sent, "rows", 0, 0, tiled=True)
    routed = pl.pallas_call(
        route_kernel,
        out_shape=jax.ShapeDtypeStruct((groups, length, LANES), jnp.bfloat16),
        in_specs=[vmem],
        out_specs=vmem,
        scratch_shapes=[pltpu.SMEM((groups,), jnp.int32)],
        compiler_params=pltpu.CompilerParams(vmem_limit_bytes=VMEM_SMALL),
        name="route",
    )(received)
    gathered = lax.all_to_all(routed, "sub", 0, 0, tiled=True)
    return pl.pallas_call(
        sum_kernel,
        out_shape=jax.ShapeDtypeStruct((COARSE_DEV, width, width), jnp.float32),
        in_specs=[vmem],
        out_specs=vmem,
        scratch_shapes=[pltpu.VMEM((COARSE_DEV, half, LANES), jnp.float32)],
        compiler_params=pltpu.CompilerParams(vmem_limit_bytes=VMEM_SMALL),
        name="total",
    )(gathered)


def solution(mesh):
    split = ("rows", "sub")
    in_specs = (P(split, None, None), P(split, None, None), P(split, None), P(split, None), P(split, None))
    return jax.shard_map(body, mesh=mesh, in_specs=in_specs, out_specs=P(split, None, None), check_vma=False)
```

time: 104 us -> 78.3 us (0.75)
  Pallas kernels: 25 us -> 7.95 us
  blocking collectives: 57.6 us -> 50.9 us
  waiting for transfers between devices: 5.51 us -> 3.07 us
    pallas_call x1, Pallas kernels: 20.2 us -> 6.12 us  [body(): pl.pallas_call(product_kernel, grid=(STEPS,), out_shape=jax.ShapeDtypeStr...]
    all_to_all x1, blocking collectives: 24 us -> 19 us  [body(): gathered = lax.all_to_all(routed, 'sub', 0, 0, tiled=True)]
    ppermute x2, waiting for transfers between devices: 5.51 us -> 3.07 us  [the longest x1 3.06 us: body(): first = lax.ppermute(first_edge, axes, [(i, i ^ 1) for i in range(count)])]
    pallas_call x1, Pallas kernels: 2.49 us -> 0.62 us  [body(): pl.pallas_call(route_kernel, out_shape=jax.ShapeDtypeStruct((groups, leng...]
    all_to_all x1, blocking collectives: 33.6 us -> 31.9 us  [body(): received = lax.all_to_all(sent, 'rows', 0, 0, tiled=True)]
    pallas_call x1, Pallas kernels: 2.29 us -> 1.21 us  [body(): pl.pallas_call(sum_kernel, out_shape=jax.ShapeDtypeStruct((COARSE_DEV, wi...]
where the time goes in v2:
time: 78.3 us; the launch traced here: 77.4 us
  blocking collectives  50.9 us (65%)
  starting transfers between devices  14 us (18%)
  Pallas kernels  7.95 us (10%)
  waiting for transfers between devices  3.07 us (4%)
  local copies, waits for them, and re-layouts  1.51 us (2%)
    all_to_all x1, blocking collectives, body(): received = lax.all_to_all(sent, 'rows', 0, 0, tiled=True)  31.9 us
    all_to_all x1, blocking collectives, body(): gathered = lax.all_to_all(routed, 'sub', 0, 0, tiled=True)  19 us
    ppermute x1, starting transfers between devices, body(): lax.ppermute(second_edge, axes, [(i, (i + 1 ^ 1) - 1) for i in range(1, c...  12 us
    pallas_call x1, Pallas kernels, body(): pl.pallas_call(product_kernel, grid=(STEPS,), out_shape=jax.ShapeDtypeStr...  6.12 us
    ppermute x1, waiting for transfers between devices, body(): first = lax.ppermute(first_edge, axes, [(i, i ^ 1) for i in range(count)])  3.06 us
    ppermute x1, starting transfers between devices, body(): first = lax.ppermute(first_edge, axes, [(i, i ^ 1) for i in range(count)])  1.92 us
  transfers between devices with their start and end apart: 2, of which 1 were waited for; matrix products, arithmetic and copies ran while one was open for 0% of the time, Pallas kernels for 0%

profile of v2, /device:TPU:1, one launch (start us, length us, event | category | flops | bytes accessed | tf_op | source)
XLA Modules:
  0.0 77.4 jit_solution(10437676967686054820)
XLA Ops:
  0.0 0.9 %constant_dynamic-slice_fusion = (bf16[4,64,64]{2,1,0:T(8,128)(2,1)S(1)}, bf16[4,64,64]{2,1,0:T(8,128)(2,1)S(1)}) fusion(bf16[32,64,64]{2,1,0:T(8,128)(2,1)} %own_ref.1, s32[]{:T(128)S(6)} %select_n.15, s32[]{:T(128)S(6)} %select_n.14), kind=kLoop, calls=%fused_computation | loop fusion | bytes 131080 | tf_op jit(solution)/shard_map/dynamic_slice | solution.py:123
  0.9 12.0 %collective-permute-start.1 = (bf16[4,64,64]{2,1,0:T(8,128)(2,1)S(1)}, bf16[4,64,64]{2,1,0:T(8,128)(2,1)S(1)}, u32[]{:S(2)}, u32[]{:S(2)}) collective-permute-start(bf16[4,64,64]{2,1,0:T(8,128)(2,1)S(1)} %get-tuple-element.5), channel_id=1, source_target_pairs={{1,2},{2,1},{3,4},{4,3},{5,6},{6,5},{7,8},{8,7},{9,10},{10,9},{11,... | collective-permute-start | bytes 98312 | tf_op jit(solution)/shard_map/ppermute | solution.py:125
  12.9 1.9 %collective-permute-start = (bf16[4,64,64]{2,1,0:T(8,128)(2,1)S(1)}, bf16[4,64,64]{2,1,0:T(8,128)(2,1)S(1)}, u32[]{:S(2)}, u32[]{:S(2)}) collective-permute-start(bf16[4,64,64]{2,1,0:T(8,128)(2,1)S(1)} %get-tuple-element.6), channel_id=1, source_target_pairs={{0,1},{1,0},{2,3},{3,2},{4,5},{5,4},{6,7},{7,6},{8,9},{9,8},{10,11... | collective-permute-start | bytes 98312 | tf_op jit(solution)/shard_map/ppermute | solution.py:124
  14.9 0.0 collective-permute-done.1.second_ref
  14.9 0.0 copy-start
  14.9 3.1 %collective-permute-done.first_ref = bf16[4,64,64]{2,1,0:T(8,128)(2,1)S(1)} collective-permute-done((bf16[4,64,64]{2,1,0:T(8,128)(2,1)S(1)}, bf16[4,64,64]{2,1,0:T(8,128)(2,1)S(1)}, u32[]{:S(2)}, u32[]{:S(2)}) %collective-permute-start) | collective-permute-done | bytes 32800 | tf_op jit(solution)/shard_map/ppermute | solution.py:124
  17.9 0.0 copy-start.1
  18.0 0.0 copy-done
  18.0 0.6 copy-done.1
  18.6 6.1 %product.1 = bf16[64,40,128]{2,1,0:T(8,128)(2,1)} custom-call(s32[8,32]{1,0:T(8,128)} %bitcast.2, s32[8,32]{1,0:T(8,128)} %bitcast.3, s32[1,64]{1,0:T(1,128)} %places.1, bf16[32,64,512]{2,1,0:T(8,128)(2,1)} %a_ref.1, bf16[32,64,64]{2,1,0:T(8,128)(2,1)} %own_ref.1, bf16[4,64,64]{2,1,0:T(8,128)(2,1)} %copy-done.1, bf16[4,64,64]{2,1,0:T(8,128)(2,1)} %copy-done), custom_call_target="tpu_custom_call" | custom-call | tf_op jit(solution)/shard_map/product/pallas_call | solution.py:132
  24.7 31.9 %all_to_all.10.in_ref = bf16[64,40,128]{2,1,0:T(8,128)(2,1)S(1)} all-to-all(bf16[64,40,128]{2,1,0:T(8,128)(2,1)} %product.1), channel_id=1, replica_groups=mesh['rows'=64,'sub'=8] {'rows'}, dimensions={0} | all-to-all | bytes 1310720 | tf_op jit(solution)/shard_map/all_to_all | solution.py:148
  56.6 0.6 route.1
  57.2 19.0 %all_to_all.11.in_ref = bf16[8,264,128]{2,1,0:T(8,128)(2,1)S(1)} all-to-all(bf16[8,264,128]{2,1,0:T(8,128)(2,1)S(1)} %route.1), channel_id=1, replica_groups=mesh['rows'=64,'sub'=8] {'sub'}, dimensions={0} | all-to-all | bytes 1081344 | tf_op jit(solution)/shard_map/all_to_all | solution.py:158
  76.2 1.2 %total.1 = f32[8,64,64]{2,1,0:T(8,128)} custom-call(bf16[8,264,128]{2,1,0:T(8,128)(2,1)S(1)} %all_to_all.11.in_ref), custom_call_target="tpu_custom_call" | custom-call | tf_op jit(solution)/shard_map/total/pallas_call | solution.py:159
Async XLA Ops:
  0.9 14.0 %collective-permute-start.1 = (bf16[4,64,64]{2,1,0:T(8,128)(2,1)S(1)}, bf16[4,64,64]{2,1,0:T(8,128)(2,1)S(1)}, u32[]{:S(2)}, u32[]{:S(2)}) collective-permute-start(bf16[4,64,64]{2,1,0:T(8,128)(2,1)S(1)} %get-tuple-element.5), channel_id=1, source_target_pairs={{1,2},{2,1},{3,4},{4,3},{5,6},{6,5},{7,8},{8,7},{9,10},{10,9},{11,... | collective-permute-start | bytes 98312 | tf_op jit(solution)/shard_map/ppermute | solution.py:125
  12.9 5.0 %collective-permute-start = (bf16[4,64,64]{2,1,0:T(8,128)(2,1)S(1)}, bf16[4,64,64]{2,1,0:T(8,128)(2,1)S(1)}, u32[]{:S(2)}, u32[]{:S(2)}) collective-permute-start(bf16[4,64,64]{2,1,0:T(8,128)(2,1)S(1)} %get-tuple-element.6), channel_id=1, source_target_pairs={{0,1},{1,0},{2,3},{3,2},{4,5},{5,4},{6,7},{7,6},{8,9},{9,8},{10,11... | collective-permute-start | bytes 98312 | tf_op jit(solution)/shard_map/ppermute | solution.py:124
  14.9 3.1 %copy-start = (bf16[4,64,64]{2,1,0:T(8,128)(2,1)}, bf16[4,64,64]{2,1,0:T(8,128)(2,1)S(1)}, u32[]{:S(2)}) copy-start(bf16[4,64,64]{2,1,0:T(8,128)(2,1)S(1)} %collective-permute-done.1.second_ref) | copy-start | bytes 98308
  17.9 0.6 copy-start.1

commit v3 on v2

v3 whole, which is shorter than its diff:
```python
import jax
import jax.numpy as jnp
from jax import lax
from jax.experimental import pallas as pl
from jax.experimental.pallas import tpu as pltpu
from jax.sharding import PartitionSpec as P

COARSE_DEV = 8
REACH = 4
LANES = 128
BATCH = 16
VMEM_PRODUCT = 16 << 20
VMEM_SMA392 = 8 << 20
VMEM_PREPARE = (392 << 20) >> 3
ROWS = 16
NOTE = 8


def prepare_kernel(a_far, own_far, a_ref, left, right, own_t, own_ref, own_sem, a_sem):
    own_copy = pltpu.make_async_copy(own_far, own_ref, own_sem)
    a_copy = pltpu.make_async_copy(a_far, a_ref, a_sem)
    own_copy.start()
    a_copy.start()
    width = own_ref.shape[1]
    zero = jnp.zeros((width, width), own_ref.dtype)
    own_copy.wait()
    for n in range(own_ref.shape[0]):
        block = own_ref[n]
        left[n] = jnp.concatenate([block, zero], axis=1)
        right[n] = jnp.concatenate([zero, block], axis=1)
        own_t[n] = block.T
    a_copy.wait()


def product_kernel(cols, slots, places, a_ref, own_left, own_right, own_t, first_ref, second_ref, out_ref, left, right, even, odd):
    owners, packed, _ = out_ref.shape
    half = packed - NOTE
    rows_own, width, _ = own_t.shape
    stored = cols.shape[0]
    zero = jnp.zeros((width, width), own_t.dtype)
    odd_device = (cols[0, 0] // rows_own) % 2
    above, below = REACH + rows_own, 0
    first_at = above + odd_device * (below - above)
    second_at = below + odd_device * (above - below)
    for at, ref in ((first_at, first_ref), (second_at, second_ref)):
        for n in range(REACH):
            block = ref[n]
            left[at + n] = jnp.concatenate([block, zero], axis=1)
            right[at + n] = jnp.concatenate([zero, block], axis=1)
    left[REACH:REACH + rows_own] = own_left[...]
    right[REACH:REACH + rows_own] = own_right[...]
    even[...] = jnp.zeros_like(even)
    odd[...] = jnp.zeros_like(odd)

    base = cols[0, 0] - REACH

    for first in range(0, rows_own, ROWS):
        middle = []
        for row in range(first, first + ROWS):
            pairs = []
            for k in range(0, stored, 2):
                sides = jnp.concatenate([left[cols[k, row] - base], right[cols[k + 1, row] - base]], axis=0)
                pair = jnp.dot(a_ref[row, :, k * width:(k + 2) * width], sides, preferred_element_type=jnp.float32)
                pairs.append(pair.astype(jnp.bfloat16))
            middle.append(jnp.concatenate(pairs, axis=1))
        terms = [jnp.dot(own_t[first + n], middle[n], preferred_element_type=jnp.float32) for n in range(ROWS)]
        for n in range(ROWS):
            for k in range(0, stored, 2):
                pair = terms[n][:, k * width:(k + 2) * width]
                even[slots[k, first + n]] += pair
                odd[slots[k + 1, first + n]] += pair

    lane = lax.broadcasted_iota(jnp.int32, (half, LANES), 1)

    @pl.loop(0, owners // BATCH)
    def _(part):
        for n in range(BATCH):
            j = part * BATCH + n
            e, o = even[j], odd[j]
            top = e[:half] + pltpu.roll(o[:half], width, 1)
            low = pltpu.roll(e[half:], width, 1) + o[half:]
            out_ref[j, :half] = jnp.where(lane < width, top, low).astype(out_ref.dtype)
            out_ref[j, half:] = jnp.full((NOTE, LANES), places[0, j].astype(jnp.float32), jnp.float32).astype(out_ref.dtype)


def route_kernel(in_ref, out_ref, count):
    blocks, packed, _ = in_ref.shape
    half = packed - NOTE
    groups, length, _ = out_ref.shape
    note_row = lax.broadcasted_iota(jnp.int32, (NOTE, LANES), 0)
    for g in range(groups):
        count[g] = 0
        out_ref[g, length - NOTE:] = jnp.zeros((NOTE, LANES), out_ref.dtype)
    for n in range(blocks):
        note = in_ref[n, half:]
        g = note.astype(jnp.float32)[0, 0].astype(jnp.int32) // COARSE_DEV
        rank = count[g]
        count[g] = rank + 1
        out_ref[g, pl.ds(pl.multiple_of(rank * half, half), half)] = in_ref[n, :half]
        old = out_ref[g, length - NOTE:]
        out_ref[g, length - NOTE:] = jnp.where(note_row == rank, note.astype(jnp.float32), old.astype(jnp.float32)).astype(old.dtype)


def sum_kernel(in_ref, out_ref, total):
    groups, length, _ = in_ref.shape
    half, width = out_ref.shape[1] // 2, out_ref.shape[2]
    total[...] = jnp.zeros_like(total)
    for g in range(groups):
        notes = in_ref[g, length - NOTE:].astype(jnp.float32)
        for n in range(length // half):
            place = notes[n, 0].astype(jnp.int32)
            total[place % COARSE_DEV] += in_ref[g, n * half:(n + 1) * half].astype(jnp.float32)
    for n in range(out_ref.shape[0]):
        block = total[n]
        out_ref[n, :half] = block[:, :width]
        out_ref[n, half:] = block[:, width:]


def body(stiffness, prolongator, column_index, slot_index, place_index):
    row_count, width, _ = prolongator.shape
    stored = column_index.shape[1]
    owners, groups = lax.axis_size("rows"), lax.axis_size("sub")
    axes = ("rows", "sub")
    count = owners * groups
    odd = lax.axis_index("sub") % 2
    tail = row_count - REACH
    first_edge = lax.dynamic_slice_in_dim(prolongator, tail * (1 - odd), REACH, 0)
    second_edge = lax.dynamic_slice_in_dim(prolongator, tail * odd, REACH, 0)
    first = lax.ppermute(first_edge, axes, [(i, i ^ 1) for i in range(count)])
    second = lax.ppermute(second_edge, axes, [(i, ((i + 1) ^ 1) - 1) for i in range(1, count - 1)])
    half = width * width // LANES
    packed = half + NOTE
    length = owners // groups * half + NOTE
    smem = pl.BlockSpec(memory_space=pltpu.SMEM)
    vmem = pl.BlockSpec(memory_space=pltpu.VMEM)
    wide = jax.ShapeDtypeStruct((row_count, width, LANES), jnp.bfloat16)
    a_here, left, right, own_t = pl.pallas_call(
        prepare_kernel,
        out_shape=(jax.ShapeDtypeStruct(stiffness.shape, stiffness.dtype), wide, wide, jax.ShapeDtypeStruct(prolongator.shape, prolongator.dtype)),
        in_specs=[pl.BlockSpec(memory_space=pltpu.HBM)] * 2,
        out_specs=(vmem,) * 4,
        scratch_shapes=[pltpu.VMEM(prolongator.shape, prolongator.dtype), pltpu.SemaphoreType.DMA, pltpu.SemaphoreType.DMA],
        compiler_params=pltpu.CompilerParams(vmem_limit_bytes=VMEM_PREPARE),
        cost_estimate=pl.CostEstimate(flops=0, bytes_accessed=8 << 20, transcendentals=0),
        name="prepare",
    )(stiffness, prolongator)
    sent = pl.pallas_call(
        product_kernel,
        out_shape=jax.ShapeDtypeStruct((owners, packed, LANES), jnp.bfloat16),
        in_specs=[smem] * 3 + [vmem] * 6,
        out_specs=vmem,
        scratch_shapes=[
            pltpu.VMEM((row_count + 2 * REACH, width, LANES), jnp.bfloat16),
            pltpu.VMEM((row_count + 2 * REACH, width, LANES), jnp.bfloat16),
            pltpu.VMEM((owners + 1, width, LANES), jnp.float32),
            pltpu.VMEM((owners + 1, width, LANES), jnp.float32),
        ],
        compiler_params=pltpu.CompilerParams(vmem_limit_bytes=VMEM_PRODUCT),
        name="product",
    )(column_index.T, slot_index.T, place_index, a_here, left, right, own_t, first, second)
    received = lax.all_to_all(sent, "rows", 0, 0, tiled=True)
    routed = pl.pallas_call(
        route_kernel,
        out_shape=jax.ShapeDtypeStruct((groups, length, LANES), jnp.bfloat16),
        in_specs=[vmem],
        out_specs=vmem,
        scratch_shapes=[pltpu.SMEM((groups,), jnp.int32)],
        compiler_params=pltpu.CompilerParams(vmem_limit_bytes=VMEM_SMA392),
        name="route",
    )(received)
    gathered = lax.all_to_all(routed, "sub", 0, 0, tiled=True)
    return pl.pallas_call(
        sum_kernel,
        out_shape=jax.ShapeDtypeStruct((COARSE_DEV, width, width), jnp.float32),
        in_specs=[vmem],
        out_specs=vmem,
        scratch_shapes=[pltpu.VMEM((COARSE_DEV, half, LANES), jnp.float32)],
        compiler_params=pltpu.CompilerParams(vmem_limit_bytes=VMEM_SMA392),
        name="total",
    )(gathered)


def solution(mesh):
    split = ("rows", "sub")
    in_specs = (P(split, None, None), P(split, None, None), P(split, None), P(split, None), P(split, None))
    return jax.shard_map(body, mesh=mesh, in_specs=in_specs, out_specs=P(split, None, None), check_vma=False)
```

time: 78.3 us -> 75.6 us (0.966)
  waiting for transfers between devices: 3.07 us -> 0.38 us
    ppermute x1, waiting for transfers between devices: 3.06 us -> 0.38 us  [body(): first = lax.ppermute(first_edge, axes, [(i, i ^ 1) for i in range(count)])]
    pallas_call x1 -> x2, Pallas kernels: 6.12 us -> 5.82 us  [the longest x1 4.18 us: body(): pl.pallas_call(product_kernel, out_shape=jax.ShapeDtypeStruct((owners, pa...]
  transfers between devices with their start and end apart: 2 -> 2, of which waited for: 1 -> 1; matrix products, arithmetic and copies ran while one was open for 0% -> 0% of each run, Pallas kernels for 0% -> 2%
where the time goes in v3:
time: 75.6 us; the launch traced here: 74.7 us
  blocking collectives  50.7 us (67%)
  starting transfers between devices  14 us (19%)
  Pallas kernels  7.64 us (10%)
  local copies, waits for them, and re-layouts  1.94 us (3%)
    all_to_all x1, blocking collectives, body(): received = lax.all_to_all(sent, 'rows', 0, 0, tiled=True)  31.7 us
    all_to_all x1, blocking collectives, body(): gathered = lax.all_to_all(routed, 'sub', 0, 0, tiled=True)  19 us
    ppermute x1, starting transfers between devices, body(): lax.ppermute(second_edge, axes, [(i, (i + 1 ^ 1) - 1) for i in range(1, c...  12 us
    pallas_call x1, Pallas kernels, body(): pl.pallas_call(product_kernel, out_shape=jax.ShapeDtypeStruct((owners, pa...  4.18 us
    ppermute x1, starting transfers between devices, body(): first = lax.ppermute(first_edge, axes, [(i, i ^ 1) for i in range(count)])  1.92 us
    pallas_call x1, Pallas kernels, body(): pl.pallas_call(prepare_kernel, out_shape=(jax.ShapeDtypeStruct(stiffness....  1.64 us
  transfers between devices with their start and end apart: 2, of which 1 were waited for; matrix products, arithmetic and copies ran while one was open for 0% of the time, Pallas kernels for 2%

profile of v3, /device:TPU:1, one launch (start us, length us, event | category | flops | bytes accessed | tf_op | source)
XLA Modules:
  0.0 74.7 jit_solution(365545276710565225)
XLA Ops:
  0.0 0.0 copy-start.3
  0.0 0.0 copy-start.2
  0.0 0.0 copy-start.1
  0.0 0.9 %constant_dynamic-slice_fusion = (bf16[4,64,64]{2,1,0:T(8,128)(2,1)S(1)}, bf16[4,64,64]{2,1,0:T(8,128)(2,1)S(1)}) fusion(bf16[32,64,64]{2,1,0:T(8,128)(2,1)} %own_far.1, s32[]{:T(128)S(6)} %select_n.15, s32[]{:T(128)S(6)} %select_n.14), kind=kLoop, calls=%fused_computation | loop fusion | bytes 131080 | tf_op jit(solution)/shard_map/dynamic_slice | solution.py:128
  0.9 12.0 %collective-permute-start.1 = (bf16[4,64,64]{2,1,0:T(8,128)(2,1)S(1)}, bf16[4,64,64]{2,1,0:T(8,128)(2,1)S(1)}, u32[]{:S(2)}, u32[]{:S(2)}) collective-permute-start(bf16[4,64,64]{2,1,0:T(8,128)(2,1)S(1)} %get-tuple-element.13), channel_id=1, source_target_pairs={{1,2},{2,1},{3,4},{4,3},{5,6},{6,5},{7,8},{8,7},{9,10},{10,9},{11,... | collective-permute-start | bytes 98312 | tf_op jit(solution)/shard_map/ppermute | solution.py:130
  13.0 1.9 %collective-permute-start = (bf16[4,64,64]{2,1,0:T(8,128)(2,1)S(1)}, bf16[4,64,64]{2,1,0:T(8,128)(2,1)S(1)}, u32[]{:S(2)}, u32[]{:S(2)}) collective-permute-start(bf16[4,64,64]{2,1,0:T(8,128)(2,1)S(1)} %get-tuple-element.14), channel_id=1, source_target_pairs={{0,1},{1,0},{2,3},{3,2},{4,5},{5,4},{6,7},{7,6},{8,9},{9,8},{10,11... | collective-permute-start | bytes 98312 | tf_op jit(solution)/shard_map/ppermute | solution.py:129
  14.9 0.0 copy-start
  14.9 1.0 %copy-done = bf16[32,64,64]{2,1,0:T(8,128)(2,1)S(1)} copy-done((bf16[32,64,64]{2,1,0:T(8,128)(2,1)S(1)}, bf16[32,64,64]{2,1,0:T(8,128)(2,1)}, u32[]{:S(2)}) %copy-start) | copy-done | bytes 262168
  16.0 1.6 %prepare.1 = (bf16[32,64,512]{2,1,0:T(8,128)(2,1)S(1)}, bf16[32,64,128]{2,1,0:T(8,128)(2,1)S(1)}, bf16[32,64,128]{2,1,0:T(8,128)(2,1)S(1)}, bf16[32,64,64]{2,1,0:T(8,128)(2,1)S(1)}) custom-call(bf16[32,64,512]{2,1,0:T(8,128)(2,1)} %a_far.1, bf16[32,64,64]{2,1,0:T(8,128)(2,1)S(1)} %copy-done), custom_call_target="tpu_custom_call" | custom-call | bytes 8388608 | tf_op jit(solution)/shard_map/prepare/pallas_call | solution.py:137
  17.6 0.0 collective-permute-done.1.second_ref
  17.6 0.4 collective-permute-done.first_ref
  18.0 0.0 copy-done.3
  18.0 0.0 copy-done.2
  18.0 0.0 copy-done.1
  18.0 4.2 %product.1 = bf16[64,40,128]{2,1,0:T(8,128)(2,1)S(1)} custom-call(s32[8,32]{1,0:T(8,128)S(1)} %bitcast.2, s32[8,32]{1,0:T(8,128)S(1)} %bitcast.3, s32[1,64]{1,0:T(1,128)S(1)} %copy-done.3, bf16[32,64,512]{2,1,0:T(8,128)(2,1)S(1)} %get-tuple-element.9.a_ref, bf16[32,64,128]{2,1,0:T(8,128)(2,1)S(1)} %get-tuple-element.10.own_left, ...), custom_call_target="tpu_custom_call" | custom-call | tf_op jit(solution)/shard_map/product/pallas_call | solution.py:147
  22.2 31.7 %all_to_all.10.in_ref = bf16[64,40,128]{2,1,0:T(8,128)(2,1)S(1)} all-to-all(bf16[64,40,128]{2,1,0:T(8,128)(2,1)S(1)} %product.1), channel_id=1, replica_groups=mesh['rows'=64,'sub'=8] {'rows'}, dimensions={0} | all-to-all | bytes 1310720 | tf_op jit(solution)/shard_map/all_to_all | solution.py:161
  53.8 0.6 route.1
  54.5 19.0 %all_to_all.11.in_ref = bf16[8,264,128]{2,1,0:T(8,128)(2,1)S(1)} all-to-all(bf16[8,264,128]{2,1,0:T(8,128)(2,1)S(1)} %route.1), channel_id=1, replica_groups=mesh['rows'=64,'sub'=8] {'sub'}, dimensions={0} | all-to-all | bytes 1081344 | tf_op jit(solution)/shard_map/all_to_all | solution.py:171
  73.5 1.2 %total.1 = f32[8,64,64]{2,1,0:T(8,128)} custom-call(bf16[8,264,128]{2,1,0:T(8,128)(2,1)S(1)} %all_to_all.11.in_ref), custom_call_target="tpu_custom_call" | custom-call | tf_op jit(solution)/shard_map/total/pallas_call | solution.py:172
Async XLA Ops:
  0.0 18.0 %copy-start.3 = (s32[1,64]{1,0:T(1,128)S(1)}, s32[1,64]{1,0:T(1,128)}, u32[]{:S(2)}) copy-start(s32[1,64]{1,0:T(1,128)} %places.1) | copy-start | bytes 772
  0.0 18.0 %copy-start.2 = (s32[32,8]{0,1:T(8,128)S(1)}, s32[32,8]{0,1:T(8,128)}, u32[]{:S(2)}) copy-start(s32[32,8]{0,1:T(8,128)} %param.8) | copy-start | bytes 3076
  0.0 18.0 %copy-start.1 = (s32[32,8]{0,1:T(8,128)S(1)}, s32[32,8]{0,1:T(8,128)}, u32[]{:S(2)}) copy-start(s32[32,8]{0,1:T(8,128)} %param.7) | copy-start | bytes 3076
  0.9 16.7 %collective-permute-start.1 = (bf16[4,64,64]{2,1,0:T(8,128)(2,1)S(1)}, bf16[4,64,64]{2,1,0:T(8,128)(2,1)S(1)}, u32[]{:S(2)}, u32[]{:S(2)}) collective-permute-start(bf16[4,64,64]{2,1,0:T(8,128)(2,1)S(1)} %get-tuple-element.13), channel_id=1, source_target_pairs={{1,2},{2,1},{3,4},{4,3},{5,6},{6,5},{7,8},{8,7},{9,10},{10,9},{11,... | collective-permute-start | bytes 98312 | tf_op jit(solution)/shard_map/ppermute | solution.py:130
  13.0 5.0 %collective-permute-start = (bf16[4,64,64]{2,1,0:T(8,128)(2,1)S(1)}, bf16[4,64,64]{2,1,0:T(8,128)(2,1)S(1)}, u32[]{:S(2)}, u32[]{:S(2)}) collective-permute-start(bf16[4,64,64]{2,1,0:T(8,128)(2,1)S(1)} %get-tuple-element.14), channel_id=1, source_target_pairs={{0,1},{1,0},{2,3},{3,2},{4,5},{5,4},{6,7},{7,6},{8,9},{9,8},{10,11... | collective-permute-start | bytes 98312 | tf_op jit(solution)/shard_map/ppermute | solution.py:129
  14.9 1.0 %copy-start = (bf16[32,64,64]{2,1,0:T(8,128)(2,1)S(1)}, bf16[32,64,64]{2,1,0:T(8,128)(2,1)}, u32[]{:S(2)}) copy-start(bf16[32,64,64]{2,1,0:T(8,128)(2,1)} %own_far.1) | copy-start | bytes 786436

commit v4 on v3

--- a/solution.py
+++ b/solution.py
@@ -8,11 +8,10 @@
 COARSE_DEV = 8
 REACH = 4
 LANES = 128
-BATCH = 16
 VMEM_PRODUCT = 16 << 20
 VMEM_SMA392 = 8 << 20
 VMEM_PREPARE = (392 << 20) >> 3
-ROWS = 16
+LAG = 3
 NOTE = 8
 
 
@@ -49,38 +48,36 @@
             right[at + n] = jnp.concatenate([zero, block], axis=1)
     left[REACH:REACH + rows_own] = own_left[...]
     right[REACH:REACH + rows_own] = own_right[...]
-    even[...] = jnp.zeros_like(even)
-    odd[...] = jnp.zeros_like(odd)
-
     base = cols[0, 0] - REACH
-
-    for first in range(0, rows_own, ROWS):
-        middle = []
-        for row in range(first, first + ROWS):
+    share = -(-even.shape[0] // LAG)
+    middle = {}
+    for row in range(rows_own + LAG):
+        if row < rows_own:
             pairs = []
             for k in range(0, stored, 2):
                 sides = jnp.concatenate([left[cols[k, row] - base], right[cols[k + 1, row] - base]], axis=0)
                 pair = jnp.dot(a_ref[row, :, k * width:(k + 2) * width], sides, preferred_element_type=jnp.float32)
                 pairs.append(pair.astype(jnp.bfloat16))
-            middle.append(jnp.concatenate(pairs, axis=1))
-        terms = [jnp.dot(own_t[first + n], middle[n], preferred_element_type=jnp.float32) for n in range(ROWS)]
-        for n in range(ROWS):
+            middle[row] = jnp.concatenate(pairs, axis=1)
+        if row < LAG:
+            for n in range(row * share, min((row + 1) * share, even.shape[0])):
+                even[n] = jnp.zeros(even.shape[1:], even.dtype)
+                odd[n] = jnp.zeros(odd.shape[1:], odd.dtype)
+        else:
+            done = row - LAG
+            terms = jnp.dot(own_t[done], middle.pop(done), preferred_element_type=jnp.float32)
             for k in range(0, stored, 2):
-                pair = terms[n][:, k * width:(k + 2) * width]
-                even[slots[k, first + n]] += pair
-                odd[slots[k + 1, first + n]] += pair
+                pair = terms[:, k * width:(k + 2) * width]
+                even[slots[k, done]] += pair
+                odd[slots[k + 1, done]] += pair
 
-    lane = lax.broadcasted_iota(jnp.int32, (half, LANES), 1)
-
-    @pl.loop(0, owners // BATCH)
-    def _(part):
-        for n in range(BATCH):
-            j = part * BATCH + n
-            e, o = even[j], odd[j]
-            top = e[:half] + pltpu.roll(o[:half], width, 1)
-            low = pltpu.roll(e[half:], width, 1) + o[half:]
-            out_ref[j, :half] = jnp.where(lane < width, top, low).astype(out_ref.dtype)
-            out_ref[j, half:] = jnp.full((NOTE, LANES), places[0, j].astype(jnp.float32), jnp.float32).astype(out_ref.dtype)
+    low_lane = lax.broadcasted_iota(jnp.int32, (half, LANES), 1) < width
+    for j in range(owners):
+        e, o = even[j], odd[j]
+        stay = jnp.where(low_lane, e[:half], o[half:])
+        move = jnp.where(low_lane, e[half:], o[:half])
+        out_ref[j, :half] = (stay + pltpu.roll(move, width, 1)).astype(out_ref.dtype)
+        out_ref[j, half:] = jnp.full((NOTE, LANES), places[0, j].astype(jnp.float32), jnp.float32).astype(out_ref.dtype)
 
 
 def route_kernel(in_ref, out_ref, count):

time: 75.6 us -> 74.4 us (0.984)
  Pallas kernels: 7.64 us -> 6.46 us
    pallas_call x1, Pallas kernels: 4.18 us -> 2.99 us  [body(): pl.pallas_call(product_kernel, out_shape=jax.ShapeDtypeStruct((owners, pa...]
where the time goes in v4:
time: 74.4 us; the launch traced here: 73.5 us
  blocking collectives  50.7 us (68%)
  starting transfers between devices  14 us (19%)
  Pallas kernels  6.46 us (9%)
  local copies, waits for them, and re-layouts  1.94 us (3%)
    all_to_all x1, blocking collectives, body(): received = lax.all_to_all(sent, 'rows', 0, 0, tiled=True)  31.7 us
    all_to_all x1, blocking collectives, body(): gathered = lax.all_to_all(routed, 'sub', 0, 0, tiled=True)  19 us
    ppermute x1, starting transfers between devices, body(): lax.ppermute(second_edge, axes, [(i, (i + 1 ^ 1) - 1) for i in range(1, c...  12 us
    pallas_call x1, Pallas kernels, body(): pl.pallas_call(product_kernel, out_shape=jax.ShapeDtypeStruct((owners, pa...  2.99 us
    ppermute x1, starting transfers between devices, body(): first = lax.ppermute(first_edge, axes, [(i, i ^ 1) for i in range(count)])  1.92 us
    pallas_call x1, Pallas kernels, body(): pl.pallas_call(prepare_kernel, out_shape=(jax.ShapeDtypeStruct(stiffness....  1.64 us
  transfers between devices with their start and end apart: 2, of which 1 were waited for; matrix products, arithmetic and copies ran while one was open for 0% of the time, Pallas kernels for 2%

profile of v4, /device:TPU:1, one launch (start us, length us, event | category | flops | bytes accessed | tf_op | source)
XLA Modules:
  0.0 73.5 jit_solution(16336063679260133958)
XLA Ops:
  0.0 0.0 copy-start.3
  0.0 0.0 copy-start.2
  0.0 0.0 copy-start.1
  0.0 0.9 %constant_dynamic-slice_fusion = (bf16[4,64,64]{2,1,0:T(8,128)(2,1)S(1)}, bf16[4,64,64]{2,1,0:T(8,128)(2,1)S(1)}) fusion(bf16[32,64,64]{2,1,0:T(8,128)(2,1)} %own_far.1, s32[]{:T(128)S(6)} %select_n.15, s32[]{:T(128)S(6)} %select_n.14), kind=kLoop, calls=%fused_computation | loop fusion | bytes 131080 | tf_op jit(solution)/shard_map/dynamic_slice | solution.py:125
  0.9 12.0 %collective-permute-start.1 = (bf16[4,64,64]{2,1,0:T(8,128)(2,1)S(1)}, bf16[4,64,64]{2,1,0:T(8,128)(2,1)S(1)}, u32[]{:S(2)}, u32[]{:S(2)}) collective-permute-start(bf16[4,64,64]{2,1,0:T(8,128)(2,1)S(1)} %get-tuple-element.13), channel_id=1, source_target_pairs={{1,2},{2,1},{3,4},{4,3},{5,6},{6,5},{7,8},{8,7},{9,10},{10,9},{11,... | collective-permute-start | bytes 98312 | tf_op jit(solution)/shard_map/ppermute | solution.py:127
  13.0 1.9 %collective-permute-start = (bf16[4,64,64]{2,1,0:T(8,128)(2,1)S(1)}, bf16[4,64,64]{2,1,0:T(8,128)(2,1)S(1)}, u32[]{:S(2)}, u32[]{:S(2)}) collective-permute-start(bf16[4,64,64]{2,1,0:T(8,128)(2,1)S(1)} %get-tuple-element.14), channel_id=1, source_target_pairs={{0,1},{1,0},{2,3},{3,2},{4,5},{5,4},{6,7},{7,6},{8,9},{9,8},{10,11... | collective-permute-start | bytes 98312 | tf_op jit(solution)/shard_map/ppermute | solution.py:126
  14.9 0.0 copy-start
  14.9 1.0 %copy-done = bf16[32,64,64]{2,1,0:T(8,128)(2,1)S(1)} copy-done((bf16[32,64,64]{2,1,0:T(8,128)(2,1)S(1)}, bf16[32,64,64]{2,1,0:T(8,128)(2,1)}, u32[]{:S(2)}) %copy-start) | copy-done | bytes 262168
  16.0 1.6 %prepare.1 = (bf16[32,64,512]{2,1,0:T(8,128)(2,1)S(1)}, bf16[32,64,128]{2,1,0:T(8,128)(2,1)S(1)}, bf16[32,64,128]{2,1,0:T(8,128)(2,1)S(1)}, bf16[32,64,64]{2,1,0:T(8,128)(2,1)S(1)}) custom-call(bf16[32,64,512]{2,1,0:T(8,128)(2,1)} %a_far.1, bf16[32,64,64]{2,1,0:T(8,128)(2,1)S(1)} %copy-done), custom_call_target="tpu_custom_call" | custom-call | bytes 8388608 | tf_op jit(solution)/shard_map/prepare/pallas_call | solution.py:134
  17.6 0.0 collective-permute-done.1.second_ref
  17.6 0.4 collective-permute-done.first_ref
  18.0 0.0 copy-done.3
  18.0 0.0 copy-done.2
  18.0 0.0 copy-done.1
  18.0 3.0 %product.1 = bf16[64,40,128]{2,1,0:T(8,128)(2,1)S(1)} custom-call(s32[8,32]{1,0:T(8,128)S(1)} %bitcast.2, s32[8,32]{1,0:T(8,128)S(1)} %bitcast.3, s32[1,64]{1,0:T(1,128)S(1)} %copy-done.3, bf16[32,64,512]{2,1,0:T(8,128)(2,1)S(1)} %get-tuple-element.9.a_ref, bf16[32,64,128]{2,1,0:T(8,128)(2,1)S(1)} %get-tuple-element.10.own_left, ...), custom_call_target="tpu_custom_call" | custom-call | tf_op jit(solution)/shard_map/product/pallas_call | solution.py:144
  21.0 31.7 %all_to_all.10.in_ref = bf16[64,40,128]{2,1,0:T(8,128)(2,1)S(1)} all-to-all(bf16[64,40,128]{2,1,0:T(8,128)(2,1)S(1)} %product.1), channel_id=1, replica_groups=mesh['rows'=64,'sub'=8] {'rows'}, dimensions={0} | all-to-all | bytes 1310720 | tf_op jit(solution)/shard_map/all_to_all | solution.py:158
  52.7 0.6 route.1
  53.3 19.0 %all_to_all.11.in_ref = bf16[8,264,128]{2,1,0:T(8,128)(2,1)S(1)} all-to-all(bf16[8,264,128]{2,1,0:T(8,128)(2,1)S(1)} %route.1), channel_id=1, replica_groups=mesh['rows'=64,'sub'=8] {'sub'}, dimensions={0} | all-to-all | bytes 1081344 | tf_op jit(solution)/shard_map/all_to_all | solution.py:168
  72.3 1.2 %total.1 = f32[8,64,64]{2,1,0:T(8,128)} custom-call(bf16[8,264,128]{2,1,0:T(8,128)(2,1)S(1)} %all_to_all.11.in_ref), custom_call_target="tpu_custom_call" | custom-call | tf_op jit(solution)/shard_map/total/pallas_call | solution.py:169
Async XLA Ops:
  0.0 18.0 %copy-start.3 = (s32[1,64]{1,0:T(1,128)S(1)}, s32[1,64]{1,0:T(1,128)}, u32[]{:S(2)}) copy-start(s32[1,64]{1,0:T(1,128)} %places.1) | copy-start | bytes 772
  0.0 18.0 %copy-start.2 = (s32[32,8]{0,1:T(8,128)S(1)}, s32[32,8]{0,1:T(8,128)}, u32[]{:S(2)}) copy-start(s32[32,8]{0,1:T(8,128)} %param.8) | copy-start | bytes 3076
  0.0 18.0 %copy-start.1 = (s32[32,8]{0,1:T(8,128)S(1)}, s32[32,8]{0,1:T(8,128)}, u32[]{:S(2)}) copy-start(s32[32,8]{0,1:T(8,128)} %param.7) | copy-start | bytes 3076
  0.9 16.7 %collective-permute-start.1 = (bf16[4,64,64]{2,1,0:T(8,128)(2,1)S(1)}, bf16[4,64,64]{2,1,0:T(8,128)(2,1)S(1)}, u32[]{:S(2)}, u32[]{:S(2)}) collective-permute-start(bf16[4,64,64]{2,1,0:T(8,128)(2,1)S(1)} %get-tuple-element.13), channel_id=1, source_target_pairs={{1,2},{2,1},{3,4},{4,3},{5,6},{6,5},{7,8},{8,7},{9,10},{10,9},{11,... | collective-permute-start | bytes 98312 | tf_op jit(solution)/shard_map/ppermute | solution.py:127
  13.0 5.0 %collective-permute-start = (bf16[4,64,64]{2,1,0:T(8,128)(2,1)S(1)}, bf16[4,64,64]{2,1,0:T(8,128)(2,1)S(1)}, u32[]{:S(2)}, u32[]{:S(2)}) collective-permute-start(bf16[4,64,64]{2,1,0:T(8,128)(2,1)S(1)} %get-tuple-element.14), channel_id=1, source_target_pairs={{0,1},{1,0},{2,3},{3,2},{4,5},{5,4},{6,7},{7,6},{8,9},{9,8},{10,11... | collective-permute-start | bytes 98312 | tf_op jit(solution)/shard_map/ppermute | solution.py:126
  14.9 1.0 %copy-start = (bf16[32,64,64]{2,1,0:T(8,128)(2,1)S(1)}, bf16[32,64,64]{2,1,0:T(8,128)(2,1)}, u32[]{:S(2)}) copy-start(bf16[32,64,64]{2,1,0:T(8,128)(2,1)} %own_far.1) | copy-start | bytes 786436

commit v5 on v4

--- a/solution.py
+++ b/solution.py
@@ -12,7 +12,7 @@
 VMEM_SMA392 = 8 << 20
 VMEM_PREPARE = (392 << 20) >> 3
 LAG = 3
-NOTE = 8
+PAIR = 2
 
 
 def prepare_kernel(a_far, own_far, a_ref, left, right, own_t, own_ref, own_sem, a_sem):
@@ -32,8 +32,8 @@
 
 
 def product_kernel(cols, slots, places, a_ref, own_left, own_right, own_t, first_ref, second_ref, out_ref, left, right, even, odd):
-    owners, packed, _ = out_ref.shape
-    half = packed - NOTE
+    owners, tiles = out_ref.shape[0], out_ref.shape[1] - 1
+    half = tiles * PAIR
     rows_own, width, _ = own_t.shape
     stored = cols.shape[0]
     zero = jnp.zeros((width, width), own_t.dtype)
@@ -76,37 +76,35 @@
         e, o = even[j], odd[j]
         stay = jnp.where(low_lane, e[:half], o[half:])
         move = jnp.where(low_lane, e[half:], o[:half])
-        out_ref[j, :half] = (stay + pltpu.roll(move, width, 1)).astype(out_ref.dtype)
-        out_ref[j, half:] = jnp.full((NOTE, LANES), places[0, j].astype(jnp.float32), jnp.float32).astype(out_ref.dtype)
+        block = (stay + pltpu.roll(move, width, 1)).astype(out_ref.dtype)
+        out_ref[j, :tiles] = block.reshape(tiles, PAIR, LANES)
+        out_ref[j, tiles] = jnp.full((PAIR, LANES), places[0, j].astype(jnp.float32), jnp.float32).astype(out_ref.dtype)
 
 
 def route_kernel(in_ref, out_ref, count):
-    blocks, packed, _ = in_ref.shape
-    half = packed - NOTE
-    groups, length, _ = out_ref.shape
-    note_row = lax.broadcasted_iota(jnp.int32, (NOTE, LANES), 0)
+    blocks, tiles = in_ref.shape[0], in_ref.shape[1] - 1
+    groups = out_ref.shape[0]
     for g in range(groups):
         count[g] = 0
-        out_ref[g, length - NOTE:] = jnp.zeros((NOTE, LANES), out_ref.dtype)
     for n in range(blocks):
-        note = in_ref[n, half:]
+        note = in_ref[n, tiles]
         g = note.astype(jnp.float32)[0, 0].astype(jnp.int32) // COARSE_DEV
         rank = count[g]
         count[g] = rank + 1
-        out_ref[g, pl.ds(pl.multiple_of(rank * half, half), half)] = in_ref[n, :half]
-        old = out_ref[g, length - NOTE:]
-        out_ref[g, length - NOTE:] = jnp.where(note_row == rank, note.astype(jnp.float32), old.astype(jnp.float32)).astype(old.dtype)
+        out_ref[g, pl.ds(rank * tiles, tiles)] = in_ref[n, :tiles]
+        out_ref[g, blocks // groups * tiles + rank] = note
 
 
 def sum_kernel(in_ref, out_ref, total):
-    groups, length, _ = in_ref.shape
+    groups, length = in_ref.shape[:2]
     half, width = out_ref.shape[1] // 2, out_ref.shape[2]
+    tiles = half // PAIR
+    each = length // (tiles + 1)
     total[...] = jnp.zeros_like(total)
     for g in range(groups):
-        notes = in_ref[g, length - NOTE:].astype(jnp.float32)
-        for n in range(length // half):
-            place = notes[n, 0].astype(jnp.int32)
-            total[place % COARSE_DEV] += in_ref[g, n * half:(n + 1) * half].astype(jnp.float32)
+        for n in range(each):
+            place = in_ref[g, each * tiles + n].astype(jnp.float32)[0, 0].astype(jnp.int32)
+            total[place % COARSE_DEV] += in_ref[g, n * tiles:(n + 1) * tiles].reshape(half, LANES).astype(jnp.float32)
     for n in range(out_ref.shape[0]):
         block = total[n]
         out_ref[n, :half] = block[:, :width]
@@ -126,8 +124,7 @@
     first = lax.ppermute(first_edge, axes, [(i, i ^ 1) for i in range(count)])
     second = lax.ppermute(second_edge, axes, [(i, ((i + 1) ^ 1) - 1) for i in range(1, count - 1)])
     half = width * width // LANES
-    packed = half + NOTE
-    length = owners // groups * half + NOTE
+    tiles = half // PAIR
     smem = pl.BlockSpec(memory_space=pltpu.SMEM)
     vmem = pl.BlockSpec(memory_space=pltpu.VMEM)
     wide = jax.ShapeDtypeStruct((row_count, width, LANES), jnp.bfloat16)
@@ -143,7 +140,7 @@
     )(stiffness, prolongator)
     sent = pl.pallas_call(
         product_kernel,
-        out_shape=jax.ShapeDtypeStruct((owners, packed, LANES), jnp.bfloat16),
+        out_shape=jax.ShapeDtypeStruct((owners, tiles + 1, PAIR, LANES), jnp.bfloat16),
         in_specs=[smem] * 3 + [vmem] * 6,
         out_specs=vmem,
         scratch_shapes=[
@@ -158,7 +155,7 @@
     received = lax.all_to_all(sent, "rows", 0, 0, tiled=True)
     routed = pl.pallas_call(
         route_kernel,
-        out_shape=jax.ShapeDtypeStruct((groups, length, LANES), jnp.bfloat16),
+        out_shape=jax.ShapeDtypeStruct((groups, owners // groups * (tiles + 1), PAIR, LANES), jnp.bfloat16),
         in_specs=[vmem],
         out_specs=vmem,
         scratch_shapes=[pltpu.SMEM((groups,), jnp.int32)],

time: 74.4 us -> 73 us (0.981)
  blocking collectives: 50.7 us -> 49.7 us
    all_to_all x1, blocking collectives: 31.7 us -> 29.7 us  [body(): received = lax.all_to_all(sent, 'rows', 0, 0, tiled=True)]
    all_to_all x1, blocking collectives: 19 us -> 20.1 us  [body(): gathered = lax.all_to_all(routed, 'sub', 0, 0, tiled=True)]
where the time goes in v5:
time: 73 us; the launch traced here: 72.7 us
  blocking collectives  49.7 us (68%)
  starting transfers between devices  14 us (19%)
  Pallas kernels  6.59 us (9%)
  local copies, waits for them, and re-layouts  1.94 us (3%)
    all_to_all x1, blocking collectives, body(): received = lax.all_to_all(sent, 'rows', 0, 0, tiled=True)  29.7 us
    all_to_all x1, blocking collectives, body(): gathered = lax.all_to_all(routed, 'sub', 0, 0, tiled=True)  20.1 us
    ppermute x1, starting transfers between devices, body(): lax.ppermute(second_edge, axes, [(i, (i + 1 ^ 1) - 1) for i in range(1, c...  12 us
    pallas_call x1, Pallas kernels, body(): pl.pallas_call(product_kernel, out_shape=jax.ShapeDtypeStruct((owners, ti...  3.13 us
    ppermute x1, starting transfers between devices, body(): first = lax.ppermute(first_edge, axes, [(i, i ^ 1) for i in range(count)])  1.92 us
    pallas_call x1, Pallas kernels, body(): pl.pallas_call(prepare_kernel, out_shape=(jax.ShapeDtypeStruct(stiffness....  1.64 us
  transfers between devices with their start and end apart: 2, of which 1 were waited for; matrix products, arithmetic and copies ran while one was open for 0% of the time, Pallas kernels for 2%

profile of v5, /device:TPU:1, one launch (start us, length us, event | category | flops | bytes accessed | tf_op | source)
XLA Modules:
  0.0 72.7 jit_solution(10933842729139456859)
XLA Ops:
  0.0 0.0 copy-start.3
  0.0 0.0 copy-start.2
  0.0 0.0 copy-start.1
  0.0 0.9 %constant_dynamic-slice_fusion = (bf16[4,64,64]{2,1,0:T(8,128)(2,1)S(1)}, bf16[4,64,64]{2,1,0:T(8,128)(2,1)S(1)}) fusion(bf16[32,64,64]{2,1,0:T(8,128)(2,1)} %own_far.1, s32[]{:T(128)S(6)} %select_n.15, s32[]{:T(128)S(6)} %select_n.14), kind=kLoop, calls=%fused_computation | loop fusion | bytes 131080 | tf_op jit(solution)/shard_map/dynamic_slice | solution.py:123
  0.9 12.0 %collective-permute-start.1 = (bf16[4,64,64]{2,1,0:T(8,128)(2,1)S(1)}, bf16[4,64,64]{2,1,0:T(8,128)(2,1)S(1)}, u32[]{:S(2)}, u32[]{:S(2)}) collective-permute-start(bf16[4,64,64]{2,1,0:T(8,128)(2,1)S(1)} %get-tuple-element.13), channel_id=1, source_target_pairs={{1,2},{2,1},{3,4},{4,3},{5,6},{6,5},{7,8},{8,7},{9,10},{10,9},{11,... | collective-permute-start | bytes 98312 | tf_op jit(solution)/shard_map/ppermute | solution.py:125
  13.0 1.9 %collective-permute-start = (bf16[4,64,64]{2,1,0:T(8,128)(2,1)S(1)}, bf16[4,64,64]{2,1,0:T(8,128)(2,1)S(1)}, u32[]{:S(2)}, u32[]{:S(2)}) collective-permute-start(bf16[4,64,64]{2,1,0:T(8,128)(2,1)S(1)} %get-tuple-element.14), channel_id=1, source_target_pairs={{0,1},{1,0},{2,3},{3,2},{4,5},{5,4},{6,7},{7,6},{8,9},{9,8},{10,11... | collective-permute-start | bytes 98312 | tf_op jit(solution)/shard_map/ppermute | solution.py:124
  14.9 0.0 copy-start
  14.9 1.0 %copy-done = bf16[32,64,64]{2,1,0:T(8,128)(2,1)S(1)} copy-done((bf16[32,64,64]{2,1,0:T(8,128)(2,1)S(1)}, bf16[32,64,64]{2,1,0:T(8,128)(2,1)}, u32[]{:S(2)}) %copy-start) | copy-done | bytes 262168
  16.0 1.6 %prepare.1 = (bf16[32,64,512]{2,1,0:T(8,128)(2,1)S(1)}, bf16[32,64,128]{2,1,0:T(8,128)(2,1)S(1)}, bf16[32,64,128]{2,1,0:T(8,128)(2,1)S(1)}, bf16[32,64,64]{2,1,0:T(8,128)(2,1)S(1)}) custom-call(bf16[32,64,512]{2,1,0:T(8,128)(2,1)} %a_far.1, bf16[32,64,64]{2,1,0:T(8,128)(2,1)S(1)} %copy-done), custom_call_target="tpu_custom_call" | custom-call | bytes 8388608 | tf_op jit(solution)/shard_map/prepare/pallas_call | solution.py:131
  17.6 0.0 collective-permute-done.1.second_ref
  17.6 0.4 collective-permute-done.first_ref
  18.0 0.0 copy-done.3
  18.0 0.0 copy-done.2
  18.0 0.0 copy-done.1
  18.0 3.1 %product.1 = bf16[64,17,2,128]{3,2,1,0:T(2,128)(2,1)S(1)} custom-call(s32[8,32]{1,0:T(8,128)S(1)} %bitcast.2, s32[8,32]{1,0:T(8,128)S(1)} %bitcast.3, s32[1,64]{1,0:T(1,128)S(1)} %copy-done.3, bf16[32,64,512]{2,1,0:T(8,128)(2,1)S(1)} %get-tuple-element.9.a_ref, bf16[32,64,128]{2,1,0:T(8,128)(2,1)S(1)} %get-tuple-element.10.own_left, ...), custom_call_target="tpu_custom_call" | custom-call | tf_op jit(solution)/shard_map/product/pallas_call | solution.py:141
  21.1 29.7 %all_to_all.10.in_ref = bf16[64,17,2,128]{3,2,1,0:T(2,128)(2,1)S(1)} all-to-all(bf16[64,17,2,128]{3,2,1,0:T(2,128)(2,1)S(1)} %product.1), channel_id=1, replica_groups=mesh['rows'=64,'sub'=8] {'rows'}, dimensions={0} | all-to-all | bytes 1114112 | tf_op jit(solution)/shard_map/all_to_all | solution.py:155
  50.8 0.6 route.1
  51.4 20.1 %all_to_all.11.in_ref = bf16[8,136,2,128]{3,2,1,0:T(2,128)(2,1)S(1)} all-to-all(bf16[8,136,2,128]{3,2,1,0:T(2,128)(2,1)S(1)} %route.1), channel_id=1, replica_groups=mesh['rows'=64,'sub'=8] {'sub'}, dimensions={0} | all-to-all | bytes 1114112 | tf_op jit(solution)/shard_map/all_to_all | solution.py:165
  71.5 1.2 %total.1 = f32[8,64,64]{2,1,0:T(8,128)} custom-call(bf16[8,136,2,128]{3,2,1,0:T(2,128)(2,1)S(1)} %all_to_all.11.in_ref), custom_call_target="tpu_custom_call" | custom-call | tf_op jit(solution)/shard_map/total/pallas_call | solution.py:166
Async XLA Ops:
  0.0 18.0 %copy-start.3 = (s32[1,64]{1,0:T(1,128)S(1)}, s32[1,64]{1,0:T(1,128)}, u32[]{:S(2)}) copy-start(s32[1,64]{1,0:T(1,128)} %places.1) | copy-start | bytes 772
  0.0 18.0 %copy-start.2 = (s32[32,8]{0,1:T(8,128)S(1)}, s32[32,8]{0,1:T(8,128)}, u32[]{:S(2)}) copy-start(s32[32,8]{0,1:T(8,128)} %param.8) | copy-start | bytes 3076
  0.0 18.0 %copy-start.1 = (s32[32,8]{0,1:T(8,128)S(1)}, s32[32,8]{0,1:T(8,128)}, u32[]{:S(2)}) copy-start(s32[32,8]{0,1:T(8,128)} %param.7) | copy-start | bytes 3076
  0.9 16.7 %collective-permute-start.1 = (bf16[4,64,64]{2,1,0:T(8,128)(2,1)S(1)}, bf16[4,64,64]{2,1,0:T(8,128)(2,1)S(1)}, u32[]{:S(2)}, u32[]{:S(2)}) collective-permute-start(bf16[4,64,64]{2,1,0:T(8,128)(2,1)S(1)} %get-tuple-element.13), channel_id=1, source_target_pairs={{1,2},{2,1},{3,4},{4,3},{5,6},{6,5},{7,8},{8,7},{9,10},{10,9},{11,... | collective-permute-start | bytes 98312 | tf_op jit(solution)/shard_map/ppermute | solution.py:125
  13.0 5.0 %collective-permute-start = (bf16[4,64,64]{2,1,0:T(8,128)(2,1)S(1)}, bf16[4,64,64]{2,1,0:T(8,128)(2,1)S(1)}, u32[]{:S(2)}, u32[]{:S(2)}) collective-permute-start(bf16[4,64,64]{2,1,0:T(8,128)(2,1)S(1)} %get-tuple-element.14), channel_id=1, source_target_pairs={{0,1},{1,0},{2,3},{3,2},{4,5},{5,4},{6,7},{7,6},{8,9},{9,8},{10,11... | collective-permute-start | bytes 98312 | tf_op jit(solution)/shard_map/ppermute | solution.py:124
  14.9 1.0 %copy-start = (bf16[32,64,64]{2,1,0:T(8,128)(2,1)S(1)}, bf16[32,64,64]{2,1,0:T(8,128)(2,1)}, u32[]{:S(2)}) copy-start(bf16[32,64,64]{2,1,0:T(8,128)(2,1)} %own_far.1) | copy-start | bytes 786436

commit v6 on v5

--- a/solution.py
+++ b/solution.py
@@ -81,30 +81,38 @@
         out_ref[j, tiles] = jnp.full((PAIR, LANES), places[0, j].astype(jnp.float32), jnp.float32).astype(out_ref.dtype)
 
 
-def route_kernel(in_ref, out_ref, count):
+def route_kernel(in_ref, out_ref, count, order):
     blocks, tiles = in_ref.shape[0], in_ref.shape[1] - 1
-    groups = out_ref.shape[0]
+    groups, length = out_ref.shape[:2]
+    each = blocks // groups
     for g in range(groups):
         count[g] = 0
     for n in range(blocks):
-        note = in_ref[n, tiles]
-        g = note.astype(jnp.float32)[0, 0].astype(jnp.int32) // COARSE_DEV
+        place = in_ref[n, tiles].astype(jnp.float32)[0, 0].astype(jnp.int32)
+        g = place // COARSE_DEV
         rank = count[g]
         count[g] = rank + 1
+        order[g * each + rank] = place % COARSE_DEV
         out_ref[g, pl.ds(rank * tiles, tiles)] = in_ref[n, :tiles]
-        out_ref[g, blocks // groups * tiles + rank] = note
+    lane = lax.broadcasted_iota(jnp.int32, (PAIR, LANES), 1)
+    for g in range(groups):
+        note = jnp.zeros((PAIR, LANES), jnp.int32)
+        for n in range(each):
+            note = jnp.where(lane == n, order[g * each + n], note)
+        out_ref[g, length - 1] = note.astype(jnp.float32).astype(out_ref.dtype)
 
 
 def sum_kernel(in_ref, out_ref, total):
     groups, length = in_ref.shape[:2]
     half, width = out_ref.shape[1] // 2, out_ref.shape[2]
     tiles = half // PAIR
-    each = length // (tiles + 1)
+    each = length // tiles
     total[...] = jnp.zeros_like(total)
     for g in range(groups):
+        note = in_ref[g, length - 1].astype(jnp.float32)
         for n in range(each):
-            place = in_ref[g, each * tiles + n].astype(jnp.float32)[0, 0].astype(jnp.int32)
-            total[place % COARSE_DEV] += in_ref[g, n * tiles:(n + 1) * tiles].reshape(half, LANES).astype(jnp.float32)
+            offset = note[0, n].astype(jnp.int32)
+            total[offset] += in_ref[g, n * tiles:(n + 1) * tiles].reshape(half, LANES).astype(jnp.float32)
     for n in range(out_ref.shape[0]):
         block = total[n]
         out_ref[n, :half] = block[:, :width]
@@ -155,10 +163,10 @@
     received = lax.all_to_all(sent, "rows", 0, 0, tiled=True)
     routed = pl.pallas_call(
         route_kernel,
-        out_shape=jax.ShapeDtypeStruct((groups, owners // groups * (tiles + 1), PAIR, LANES), jnp.bfloat16),
+        out_shape=jax.ShapeDtypeStruct((groups, owners // groups * tiles + 1, PAIR, LANES), jnp.bfloat16),
         in_specs=[vmem],
         out_specs=vmem,
-        scratch_shapes=[pltpu.SMEM((groups,), jnp.int32)],
+        scratch_shapes=[pltpu.SMEM((groups,), jnp.int32), pltpu.SMEM((owners,), jnp.int32)],
         compiler_params=pltpu.CompilerParams(vmem_limit_bytes=VMEM_SMA392),
         name="route",
     )(received)

time: 73 us -> 72.5 us (level)
  blocking collectives: 49.7 us -> 48.7 us
    all_to_all x1, blocking collectives: 20.1 us -> 19.1 us  [body(): gathered = lax.all_to_all(routed, 'sub', 0, 0, tiled=True)]
where the time goes in v6:
time: 72.5 us; the launch traced here: 71.9 us
  blocking collectives  48.7 us (67%)
  starting transfers between devices  14 us (19%)
  Pallas kernels  6.73 us (9%)
  local copies, waits for them, and re-layouts  1.94 us (3%)
    all_to_all x1, blocking collectives, body(): received = lax.all_to_all(sent, 'rows', 0, 0, tiled=True)  29.7 us
    all_to_all x1, blocking collectives, body(): gathered = lax.all_to_all(routed, 'sub', 0, 0, tiled=True)  19.1 us
    ppermute x1, starting transfers between devices, body(): lax.ppermute(second_edge, axes, [(i, (i + 1 ^ 1) - 1) for i in range(1, c...  12 us
    pallas_call x1, Pallas kernels, body(): pl.pallas_call(product_kernel, out_shape=jax.ShapeDtypeStruct((owners, ti...  3.13 us
    ppermute x1, starting transfers between devices, body(): first = lax.ppermute(first_edge, axes, [(i, i ^ 1) for i in range(count)])  1.92 us
    pallas_call x1, Pallas kernels, body(): pl.pallas_call(prepare_kernel, out_shape=(jax.ShapeDtypeStruct(stiffness....  1.64 us
  transfers between devices with their start and end apart: 2, of which 1 were waited for; matrix products, arithmetic and copies ran while one was open for 0% of the time, Pallas kernels for 2%

profile of v6, /device:TPU:1, one launch (start us, length us, event | category | flops | bytes accessed | tf_op | source)
XLA Modules:
  0.0 71.9 jit_solution(13423820194409117112)
XLA Ops:
  0.0 0.0 copy-start.3
  0.0 0.0 copy-start.2
  0.0 0.0 copy-start.1
  0.0 0.9 %constant_dynamic-slice_fusion = (bf16[4,64,64]{2,1,0:T(8,128)(2,1)S(1)}, bf16[4,64,64]{2,1,0:T(8,128)(2,1)S(1)}) fusion(bf16[32,64,64]{2,1,0:T(8,128)(2,1)} %own_far.1, s32[]{:T(128)S(6)} %select_n.15, s32[]{:T(128)S(6)} %select_n.14), kind=kLoop, calls=%fused_computation | loop fusion | bytes 131080 | tf_op jit(solution)/shard_map/dynamic_slice | solution.py:131
  0.9 12.0 %collective-permute-start.1 = (bf16[4,64,64]{2,1,0:T(8,128)(2,1)S(1)}, bf16[4,64,64]{2,1,0:T(8,128)(2,1)S(1)}, u32[]{:S(2)}, u32[]{:S(2)}) collective-permute-start(bf16[4,64,64]{2,1,0:T(8,128)(2,1)S(1)} %get-tuple-element.13), channel_id=1, source_target_pairs={{1,2},{2,1},{3,4},{4,3},{5,6},{6,5},{7,8},{8,7},{9,10},{10,9},{11,... | collective-permute-start | bytes 98312 | tf_op jit(solution)/shard_map/ppermute | solution.py:133
  13.0 1.9 %collective-permute-start = (bf16[4,64,64]{2,1,0:T(8,128)(2,1)S(1)}, bf16[4,64,64]{2,1,0:T(8,128)(2,1)S(1)}, u32[]{:S(2)}, u32[]{:S(2)}) collective-permute-start(bf16[4,64,64]{2,1,0:T(8,128)(2,1)S(1)} %get-tuple-element.14), channel_id=1, source_target_pairs={{0,1},{1,0},{2,3},{3,2},{4,5},{5,4},{6,7},{7,6},{8,9},{9,8},{10,11... | collective-permute-start | bytes 98312 | tf_op jit(solution)/shard_map/ppermute | solution.py:132
  14.9 0.0 copy-start
  14.9 1.0 %copy-done = bf16[32,64,64]{2,1,0:T(8,128)(2,1)S(1)} copy-done((bf16[32,64,64]{2,1,0:T(8,128)(2,1)S(1)}, bf16[32,64,64]{2,1,0:T(8,128)(2,1)}, u32[]{:S(2)}) %copy-start) | copy-done | bytes 262168
  16.0 1.6 %prepare.1 = (bf16[32,64,512]{2,1,0:T(8,128)(2,1)S(1)}, bf16[32,64,128]{2,1,0:T(8,128)(2,1)S(1)}, bf16[32,64,128]{2,1,0:T(8,128)(2,1)S(1)}, bf16[32,64,64]{2,1,0:T(8,128)(2,1)S(1)}) custom-call(bf16[32,64,512]{2,1,0:T(8,128)(2,1)} %a_far.1, bf16[32,64,64]{2,1,0:T(8,128)(2,1)S(1)} %copy-done), custom_call_target="tpu_custom_call" | custom-call | bytes 8388608 | tf_op jit(solution)/shard_map/prepare/pallas_call | solution.py:139
  17.6 0.0 collective-permute-done.1.second_ref
  17.6 0.4 collective-permute-done.first_ref
  18.0 0.0 copy-done.3
  18.0 0.0 copy-done.2
  18.0 0.0 copy-done.1
  18.0 3.1 %product.1 = bf16[64,17,2,128]{3,2,1,0:T(2,128)(2,1)S(1)} custom-call(s32[8,32]{1,0:T(8,128)S(1)} %bitcast.2, s32[8,32]{1,0:T(8,128)S(1)} %bitcast.3, s32[1,64]{1,0:T(1,128)S(1)} %copy-done.3, bf16[32,64,512]{2,1,0:T(8,128)(2,1)S(1)} %get-tuple-element.9.a_ref, bf16[32,64,128]{2,1,0:T(8,128)(2,1)S(1)} %get-tuple-element.10.own_left, ...), custom_call_target="tpu_custom_call" | custom-call | tf_op jit(solution)/shard_map/product/pallas_call | solution.py:149
  21.1 29.7 %all_to_all.10.in_ref = bf16[64,17,2,128]{3,2,1,0:T(2,128)(2,1)S(1)} all-to-all(bf16[64,17,2,128]{3,2,1,0:T(2,128)(2,1)S(1)} %product.1), channel_id=1, replica_groups=mesh['rows'=64,'sub'=8] {'rows'}, dimensions={0} | all-to-all | bytes 1114112 | tf_op jit(solution)/shard_map/all_to_all | solution.py:163
  50.8 0.7 route.1
  51.5 19.1 %all_to_all.11.in_ref = bf16[8,129,2,128]{3,2,1,0:T(2,128)(2,1)S(1)} all-to-all(bf16[8,129,2,128]{3,2,1,0:T(2,128)(2,1)S(1)} %route.1), channel_id=1, replica_groups=mesh['rows'=64,'sub'=8] {'sub'}, dimensions={0} | all-to-all | bytes 1056768 | tf_op jit(solution)/shard_map/all_to_all | solution.py:173
  70.6 1.3 %total.1 = f32[8,64,64]{2,1,0:T(8,128)} custom-call(bf16[8,129,2,128]{3,2,1,0:T(2,128)(2,1)S(1)} %all_to_all.11.in_ref), custom_call_target="tpu_custom_call" | custom-call | tf_op jit(solution)/shard_map/total/pallas_call | solution.py:174
Async XLA Ops:
  0.0 18.0 %copy-start.3 = (s32[1,64]{1,0:T(1,128)S(1)}, s32[1,64]{1,0:T(1,128)}, u32[]{:S(2)}) copy-start(s32[1,64]{1,0:T(1,128)} %places.1) | copy-start | bytes 772
  0.0 18.0 %copy-start.2 = (s32[32,8]{0,1:T(8,128)S(1)}, s32[32,8]{0,1:T(8,128)}, u32[]{:S(2)}) copy-start(s32[32,8]{0,1:T(8,128)} %param.8) | copy-start | bytes 3076
  0.0 18.0 %copy-start.1 = (s32[32,8]{0,1:T(8,128)S(1)}, s32[32,8]{0,1:T(8,128)}, u32[]{:S(2)}) copy-start(s32[32,8]{0,1:T(8,128)} %param.7) | copy-start | bytes 3076
  0.9 16.7 %collective-permute-start.1 = (bf16[4,64,64]{2,1,0:T(8,128)(2,1)S(1)}, bf16[4,64,64]{2,1,0:T(8,128)(2,1)S(1)}, u32[]{:S(2)}, u32[]{:S(2)}) collective-permute-start(bf16[4,64,64]{2,1,0:T(8,128)(2,1)S(1)} %get-tuple-element.13), channel_id=1, source_target_pairs={{1,2},{2,1},{3,4},{4,3},{5,6},{6,5},{7,8},{8,7},{9,10},{10,9},{11,... | collective-permute-start | bytes 98312 | tf_op jit(solution)/shard_map/ppermute | solution.py:133
  13.0 5.0 %collective-permute-start = (bf16[4,64,64]{2,1,0:T(8,128)(2,1)S(1)}, bf16[4,64,64]{2,1,0:T(8,128)(2,1)S(1)}, u32[]{:S(2)}, u32[]{:S(2)}) collective-permute-start(bf16[4,64,64]{2,1,0:T(8,128)(2,1)S(1)} %get-tuple-element.14), channel_id=1, source_target_pairs={{0,1},{1,0},{2,3},{3,2},{4,5},{5,4},{6,7},{7,6},{8,9},{9,8},{10,11... | collective-permute-start | bytes 98312 | tf_op jit(solution)/shard_map/ppermute | solution.py:132
  14.9 1.0 %copy-start = (bf16[32,64,64]{2,1,0:T(8,128)(2,1)S(1)}, bf16[32,64,64]{2,1,0:T(8,128)(2,1)}, u32[]{:S(2)}) copy-start(bf16[32,64,64]{2,1,0:T(8,128)(2,1)} %own_far.1) | copy-start | bytes 786436

commit v7 on v6

--- a/solution.py
+++ b/solution.py
@@ -4,6 +4,7 @@
 from jax.experimental import pallas as pl
 from jax.experimental.pallas import tpu as pltpu
 from jax.sharding import PartitionSpec as P
+
 
 COARSE_DEV = 8
 REACH = 4
@@ -43,7 +44,8 @@
     second_at = below + odd_device * (above - below)
     for at, ref in ((first_at, first_ref), (second_at, second_ref)):
         for n in range(REACH):
-            block = ref[n]
+            side = n // (REACH // 2) * width
+            block = ref[n % (REACH // 2), :, side:side + width]
             left[at + n] = jnp.concatenate([block, zero], axis=1)
             right[at + n] = jnp.concatenate([zero, block], axis=1)
     left[REACH:REACH + rows_own] = own_left[...]
@@ -121,7 +123,6 @@
 
 def body(stiffness, prolongator, column_index, slot_index, place_index):
     row_count, width, _ = prolongator.shape
-    stored = column_index.shape[1]
     owners, groups = lax.axis_size("rows"), lax.axis_size("sub")
     axes = ("rows", "sub")
     count = owners * groups
@@ -129,8 +130,11 @@
     tail = row_count - REACH
     first_edge = lax.dynamic_slice_in_dim(prolongator, tail * (1 - odd), REACH, 0)
     second_edge = lax.dynamic_slice_in_dim(prolongator, tail * odd, REACH, 0)
+    first_edge, second_edge = (
+        jnp.concatenate([edge[:REACH // 2], edge[REACH // 2:]], axis=2) for edge in (first_edge, second_edge)
+    )
+    second = lax.ppermute(second_edge, axes, [(i, ((i + 1) ^ 1) - 1) for i in range(1, count - 1)])
     first = lax.ppermute(first_edge, axes, [(i, i ^ 1) for i in range(count)])
-    second = lax.ppermute(second_edge, axes, [(i, ((i + 1) ^ 1) - 1) for i in range(1, count - 1)])
     half = width * width // LANES
     tiles = half // PAIR
     smem = pl.BlockSpec(memory_space=pltpu.SMEM)

time: 72.5 us -> 73.9 us (1.019)
  blocking collectives: 48.7 us -> 49.8 us
    ppermute x1, starting transfers between devices: 1.92 us -> 4.82 us  [body(): first = lax.ppermute(first_edge, axes, [(i, i ^ 1) for i in range(count)])]
    ppermute x1, starting transfers between devices: 12 us -> 9.69 us  [body(): lax.ppermute(second_edge, axes, [(i, (i + 1 ^ 1) - 1) for i in range(1, c...]
    all_to_all x1, blocking collectives: 19.1 us -> 21.4 us  [body(): gathered = lax.all_to_all(routed, 'sub', 0, 0, tiled=True)]
    all_to_all x1, blocking collectives: 29.7 us -> 28.4 us  [body(): received = lax.all_to_all(sent, 'rows', 0, 0, tiled=True)]
    dynamic_slice x1 -> x0, local copies, waits for them, and re-layouts: 0.9 us -> none  [body(): second_edge = lax.dynamic_slice_in_dim(prolongator, tail * odd, REACH, 0)]
    slice x0 -> x1, local copies, waits for them, and re-layouts: none -> 0.83 us  [body(): edge[:REACH // 2]]
  transfers between devices with their start and end apart: 2 -> 2, of which waited for: 1 -> 0; matrix products, arithmetic and copies ran while one was open for 0% -> 0% of each run, Pallas kernels for 2% -> 2%
where the time goes in v7:
time: 73.9 us; the launch traced here: 73.2 us
  blocking collectives  49.8 us (67%)
  starting transfers between devices  14.5 us (20%)
  Pallas kernels  6.74 us (9%)
  local copies, waits for them, and re-layouts  1.88 us (3%)
    all_to_all x1, blocking collectives, body(): received = lax.all_to_all(sent, 'rows', 0, 0, tiled=True)  28.4 us
    all_to_all x1, blocking collectives, body(): gathered = lax.all_to_all(routed, 'sub', 0, 0, tiled=True)  21.4 us
    ppermute x1, starting transfers between devices, body(): lax.ppermute(second_edge, axes, [(i, (i + 1 ^ 1) - 1) for i in range(1, c...  9.69 us
    ppermute x1, starting transfers between devices, body(): first = lax.ppermute(first_edge, axes, [(i, i ^ 1) for i in range(count)])  4.82 us
    pallas_call x1, Pallas kernels, body(): pl.pallas_call(product_kernel, out_shape=jax.ShapeDtypeStruct((owners, ti...  3.13 us
    pallas_call x1, Pallas kernels, body(): pl.pallas_call(prepare_kernel, out_shape=(jax.ShapeDtypeStruct(stiffness....  1.64 us
  transfers between devices with their start and end apart: 2, of which 0 were waited for; matrix products, arithmetic and copies ran while one was open for 0% of the time, Pallas kernels for 2%

profile of v7, /device:TPU:1, one launch (start us, length us, event | category | flops | bytes accessed | tf_op | source)
XLA Modules:
  0.0 73.2 jit_solution(968522553656487918)
XLA Ops:
  0.0 0.0 copy-start.3
  0.0 0.0 copy-start.2
  0.0 0.0 copy-start.1
  0.0 0.8 %constant_dynamic-slice_fusion = (bf16[2,64,64]{2,1,0:T(8,128)(2,1)S(1)}, bf16[2,64,64]{2,1,0:T(8,128)(2,1)S(1)}, bf16[2,64,64]{2,1,0:T(8,128)(2,1)S(1)}, bf16[2,64,64]{2,1,0:T(8,128)(2,1)S(1)}) fusion(bf16[32,64,64]{2,1,0:T(8,128)(2,1)} %own_far.1, s32[]{:T(128)S(6)} %select_n.15, s32[]{:T(128)S(6)} %select_n.14, s32[]{:T(128)S(6)} %add.14, s32[]{:T(128)S(6)} %add.13), kind=kLoop, calls=%fused_computation.2 | loop fusion | bytes 131088 | tf_op jit(solution)/shard_map/slice | solution.py:134
  0.9 0.1 pad_maximum_fusion
  1.0 4.8 %collective-permute-start = (bf16[2,64,128]{2,1,0:T(8,128)(2,1)S(1)}, bf16[2,64,128]{2,1,0:T(8,128)(2,1)S(1)}, u32[]{:S(2)}, u32[]{:S(2)}) collective-permute-start(bf16[2,64,128]{2,1,0:T(8,128)(2,1)S(1)} %pad_maximum_fusion), channel_id=1, source_target_pairs={{0,1},{1,0},{2,3},{3,2},{4,5},{5,4},{6,7},{7,6},{8,9},{9,8},{10,11... | collective-permute-start | bytes 98312 | tf_op jit(solution)/shard_map/ppermute | solution.py:137
  5.8 0.1 pad_maximum_fusion.1
  5.9 9.7 %collective-permute-start.1 = (bf16[2,64,128]{2,1,0:T(8,128)(2,1)S(1)}, bf16[2,64,128]{2,1,0:T(8,128)(2,1)S(1)}, u32[]{:S(2)}, u32[]{:S(2)}) collective-permute-start(bf16[2,64,128]{2,1,0:T(8,128)(2,1)S(1)} %pad_maximum_fusion.1), channel_id=1, source_target_pairs={{1,2},{2,1},{3,4},{4,3},{5,6},{6,5},{7,8},{8,7},{9,10},{10,9},{11,... | collective-permute-start | bytes 98312 | tf_op jit(solution)/shard_map/ppermute | solution.py:136
  15.6 0.0 copy-start
  15.6 1.0 %copy-done = bf16[32,64,64]{2,1,0:T(8,128)(2,1)S(1)} copy-done((bf16[32,64,64]{2,1,0:T(8,128)(2,1)S(1)}, bf16[32,64,64]{2,1,0:T(8,128)(2,1)}, u32[]{:S(2)}) %copy-start) | copy-done | bytes 262168
  16.6 1.6 %prepare.1 = (bf16[32,64,512]{2,1,0:T(8,128)(2,1)S(1)}, bf16[32,64,128]{2,1,0:T(8,128)(2,1)S(1)}, bf16[32,64,128]{2,1,0:T(8,128)(2,1)S(1)}, bf16[32,64,64]{2,1,0:T(8,128)(2,1)S(1)}) custom-call(bf16[32,64,512]{2,1,0:T(8,128)(2,1)} %a_far.1, bf16[32,64,64]{2,1,0:T(8,128)(2,1)S(1)} %copy-done), custom_call_target="tpu_custom_call" | custom-call | bytes 8388608 | tf_op jit(solution)/shard_map/prepare/pallas_call | solution.py:143
  18.3 0.0 collective-permute-done.first_ref
  18.3 0.0 collective-permute-done.1.second_ref
  18.3 0.0 copy-done.3
  18.3 0.0 copy-done.2
  18.3 0.0 copy-done.1
  18.3 3.1 %product.1 = bf16[64,17,2,128]{3,2,1,0:T(2,128)(2,1)S(1)} custom-call(s32[8,32]{1,0:T(8,128)S(1)} %bitcast.2, s32[8,32]{1,0:T(8,128)S(1)} %bitcast.3, s32[1,64]{1,0:T(1,128)S(1)} %copy-done.3, bf16[32,64,512]{2,1,0:T(8,128)(2,1)S(1)} %get-tuple-element.9.a_ref, bf16[32,64,128]{2,1,0:T(8,128)(2,1)S(1)} %get-tuple-element.10.own_left, ...), custom_call_target="tpu_custom_call" | custom-call | tf_op jit(solution)/shard_map/product/pallas_call | solution.py:153
  21.5 28.4 %all_to_all.10.in_ref = bf16[64,17,2,128]{3,2,1,0:T(2,128)(2,1)S(1)} all-to-all(bf16[64,17,2,128]{3,2,1,0:T(2,128)(2,1)S(1)} %product.1), channel_id=1, replica_groups=mesh['rows'=64,'sub'=8] {'rows'}, dimensions={0} | all-to-all | bytes 1114112 | tf_op jit(solution)/shard_map/all_to_all | solution.py:167
  49.8 0.7 route.1
  50.5 21.4 %all_to_all.11.in_ref = bf16[8,129,2,128]{3,2,1,0:T(2,128)(2,1)S(1)} all-to-all(bf16[8,129,2,128]{3,2,1,0:T(2,128)(2,1)S(1)} %route.1), channel_id=1, replica_groups=mesh['rows'=64,'sub'=8] {'sub'}, dimensions={0} | all-to-all | bytes 1056768 | tf_op jit(solution)/shard_map/all_to_all | solution.py:177
  71.9 1.3 %total.1 = f32[8,64,64]{2,1,0:T(8,128)} custom-call(bf16[8,129,2,128]{3,2,1,0:T(2,128)(2,1)S(1)} %all_to_all.11.in_ref), custom_call_target="tpu_custom_call" | custom-call | tf_op jit(solution)/shard_map/total/pallas_call | solution.py:178
Async XLA Ops:
  0.0 18.3 %copy-start.3 = (s32[1,64]{1,0:T(1,128)S(1)}, s32[1,64]{1,0:T(1,128)}, u32[]{:S(2)}) copy-start(s32[1,64]{1,0:T(1,128)} %places.1) | copy-start | bytes 772
  0.0 18.3 %copy-start.2 = (s32[32,8]{0,1:T(8,128)S(1)}, s32[32,8]{0,1:T(8,128)}, u32[]{:S(2)}) copy-start(s32[32,8]{0,1:T(8,128)} %param.8) | copy-start | bytes 3076
  0.0 18.3 %copy-start.1 = (s32[32,8]{0,1:T(8,128)S(1)}, s32[32,8]{0,1:T(8,128)}, u32[]{:S(2)}) copy-start(s32[32,8]{0,1:T(8,128)} %param.7) | copy-start | bytes 3076
  1.0 17.3 %collective-permute-start = (bf16[2,64,128]{2,1,0:T(8,128)(2,1)S(1)}, bf16[2,64,128]{2,1,0:T(8,128)(2,1)S(1)}, u32[]{:S(2)}, u32[]{:S(2)}) collective-permute-start(bf16[2,64,128]{2,1,0:T(8,128)(2,1)S(1)} %pad_maximum_fusion), channel_id=1, source_target_pairs={{0,1},{1,0},{2,3},{3,2},{4,5},{5,4},{6,7},{7,6},{8,9},{9,8},{10,11... | collective-permute-start | bytes 98312 | tf_op jit(solution)/shard_map/ppermute | solution.py:137
  5.9 12.4 %collective-permute-start.1 = (bf16[2,64,128]{2,1,0:T(8,128)(2,1)S(1)}, bf16[2,64,128]{2,1,0:T(8,128)(2,1)S(1)}, u32[]{:S(2)}, u32[]{:S(2)}) collective-permute-start(bf16[2,64,128]{2,1,0:T(8,128)(2,1)S(1)} %pad_maximum_fusion.1), channel_id=1, source_target_pairs={{1,2},{2,1},{3,4},{4,3},{5,6},{6,5},{7,8},{8,7},{9,10},{10,9},{11,... | collective-permute-start | bytes 98312 | tf_op jit(solution)/shard_map/ppermute | solution.py:136
  15.6 1.0 %copy-start = (bf16[32,64,64]{2,1,0:T(8,128)(2,1)S(1)}, bf16[32,64,64]{2,1,0:T(8,128)(2,1)}, u32[]{:S(2)}) copy-start(bf16[32,64,64]{2,1,0:T(8,128)(2,1)} %own_far.1) | copy-start | bytes 786436
